TPU v7x, 32 devices: a whole 2x2x4 slice. The times are simulated.
32 devices in a mesh: dp: 4 (over z), ctx: 4 (over x, core), fsdp: 2 (over y).
Axes of the slice: x: 2, y: 2, z: 4, core: 2. Of those that a mesh axis runs over, the one named last changes fastest.
Arguments:
- states: bfloat16 [32, 512, 1024], P(('dp', 'fsdp'), 'ctx'), may hold values from -6 to 6
- cotangent: bfloat16 [32, 512, 1024], P(('dp', 'fsdp'), 'ctx'), may hold values from -6 to 6
- lengths: int32 [32], replicated, may hold values from 128 to 512, as said below
- slot_source: int32 [32], replicated, may hold values from 0 to 31, as said below
- query_weight: bfloat16 [1024, 1024], P('fsdp'), may hold values from -0.1875 to 0.1875
- query_bias: bfloat16 [1024], P('fsdp'), may hold values from -3 to 3
- key_weight: bfloat16 [1024, 1024], P('fsdp'), may hold values from -0.1875 to 0.1875
- value_weight: bfloat16 [1024, 1024], P('fsdp'), may hold values from -0.1875 to 0.1875
- value_bias: bfloat16 [1024], P('fsdp'), may hold values from -3 to 3
- output_weight: bfloat16 [1024, 1024], P('fsdp'), may hold values from -0.5 to 0.5
- output_bias: bfloat16 [1024], P('fsdp'), may hold values from -3 to 3
- first_gain: bfloat16 [1024], P('fsdp'), may hold values from 0.5 to 1.5
- first_shift: bfloat16 [1024], P('fsdp'), may hold values from -3 to 3
- inner_weight: bfloat16 [1024, 4096], P('fsdp'), may hold values from -0.1875 to 0.1875
- inner_bias: bfloat16 [4096], P('fsdp'), may hold values from -3 to 3
- outer_weight: bfloat16 [4096, 1024], P('fsdp'), may hold values from -0.09375 to 0.09375
- outer_bias: bfloat16 [1024], P('fsdp'), may hold values from -3 to 3
- final_gain: bfloat16 [1024], P('fsdp'), may hold values from 0.5 to 1.5
- final_shift: bfloat16 [1024], P('fsdp'), may hold values from -3 to 3
Outputs:
- encoded: bfloat16 [32, 512, 1024], P(('dp', 'fsdp'), 'ctx')
- input_grad: bfloat16 [32, 512, 1024], P(('dp', 'fsdp'), 'ctx')
- query_weight_grad: float32 [1024, 1024], P(('dp', 'ctx', 'fsdp'))
- query_bias_grad: float32 [1024], P(('dp', 'ctx', 'fsdp'))
- key_weight_grad: float32 [1024, 1024], P(('dp', 'ctx', 'fsdp'))
- value_weight_grad: float32 [1024, 1024], P(('dp', 'ctx', 'fsdp'))
- value_bias_grad: float32 [1024], P(('dp', 'ctx', 'fsdp'))
- output_weight_grad: float32 [1024, 1024], P(('dp', 'ctx', 'fsdp'))
- output_bias_grad: float32 [1024], P(('dp', 'ctx', 'fsdp'))
- first_gain_grad: float32 [1024], P(('dp', 'ctx', 'fsdp'))
- first_shift_grad: float32 [1024], P(('dp', 'ctx', 'fsdp'))
- inner_weight_grad: float32 [1024, 4096], P(('dp', 'ctx', 'fsdp'))
- inner_bias_grad: float32 [4096], P(('dp', 'ctx', 'fsdp'))
- outer_weight_grad: float32 [4096, 1024], P(('dp', 'ctx', 'fsdp'))
- outer_bias_gradient: float32 [1024], P(('dp', 'ctx', 'fsdp'))
- final_gain_grad: float32 [1024], P(('dp', 'ctx', 'fsdp'))
- final_shift_grad: float32 [1024], P(('dp', 'ctx', 'fsdp'))
Inputs may be any that keep to these rules, and one draw needn't show every extreme that they name: slot_source is a permutation of the 32 sequences. Slot t belongs to group t // 8; the 4 slots of one index of dp and fsdp (an aligned block) take their sequences from the devices of the same index of fsdp whose groups lie in the same aligned set of four groups, 1 from each of the four. `lengths`: every aligned block of 4 slots holds one sequence of 512 tokens, and the valid tokens of two such blocks differ by at most 192.
All inputs are finite; a program needn't handle non-finite values.
Results may differ from a plain program's by a relative error of at most 0.015.
Values may be sent and summed in bfloat16 or wider, within the bound.
A program may use at most 192 MiB of HBM per device.

v0:
```python
import functools
import math

import jax
import jax.numpy as jnp
from jax import lax
from jax.experimental import pallas as pl
from jax.experimental.pallas import tpu as pltpu
from jax.sharding import PartitionSpec as P

HEADS = 16
EPS = 1e-12
MASKED = -1e30
F32 = jnp.float32
BF16 = jnp.bfloat16
OWNERS = ("dp", "ctx", "fsdp")


def swap(value, axis, mask):
    pairs = [(source, source ^ mask) for source in range(lax.axis_size(axis))]
    return lax.ppermute(value, axis, pairs)


def pick(array, index, axis):
    return lax.dynamic_index_in_dim(array, index, axis, keepdims=False)


def add_low(left, right):
    return (left.astype(F32) + right.astype(F32)).astype(BF16)


def matmul(left, right):
    return jnp.dot(left, right, preferred_element_type=F32)


def matmul_tn(left, right):
    return lax.dot_general(left, right, (((0,), (0,)), ((), ())), preferred_element_type=F32)


def matmul_nt(left, right):
    return lax.dot_general(left, right, (((1,), (1,)), ((), ())), preferred_element_type=F32)


def col_sum(matrix):
    return jnp.sum(matrix.astype(F32), axis=0)


def norm_rows(summed, scale_vec, shift_vec):
    row_mean = jnp.mean(summed, axis=-1, keepdims=True)
    centered = summed - row_mean
    inverse = lax.rsqrt(jnp.mean(centered * centered, axis=-1, keepdims=True) + EPS)
    normed = centered * inverse
    return (normed * scale_vec + shift_vec, normed, inverse)


def norm_back(upstream, normed, inverse, scale_vec):
    scaled = upstream * scale_vec
    return inverse * (
        scaled
        - jnp.mean(scaled, axis=-1, keepdims=True)
        - normed * jnp.mean(scaled * normed, axis=-1, keepdims=True)
    )


def half_lanes(pair, which):
    lane = lax.broadcasted_iota(jnp.int32, pair.shape, 1)
    keep = lane < 64 if which == 0 else lane >= 64
    return jnp.where(keep, pair, jnp.zeros_like(pair))


def with_flag(pair, flag, which):
    lane = lax.broadcasted_iota(jnp.int32, pair.shape, 1)
    keep = lane < 64 if which == 0 else lane >= 64
    spot = lane == (64 if which == 0 else 0)
    return jnp.where(keep, pair, jnp.where(spot, flag, jnp.zeros_like(pair)))


def attend_kernel(qkv_ref, bias_ref, out_ref, lse_ref):
    width = out_ref.shape[-1]
    rows = out_ref.shape[0] * out_ref.shape[2]
    bias = bias_ref[0]
    lane = lax.broadcasted_iota(jnp.int32, (rows, 128), 1)
    one = jnp.ones((rows, 128), BF16)
    totals = jnp.zeros((rows, 128), F32)
    for pair_index in range(width // 128):
        first = pair_index * 128
        query = qkv_ref[:, 0, :, first : first + 128].reshape(rows, 128)
        key = qkv_ref[:, 0, :, width + first : width + first + 128].reshape(rows, 128)
        value = qkv_ref[:, 0, :, 2 * width + first : 2 * width + first + 128].reshape(rows, 128)
        query = (query.astype(F32) * 0.125).astype(BF16)
        mixed = []
        for which in range(2):
            scores = matmul_nt(with_flag(query, one, which), with_flag(key, bias, which))
            top = jnp.max(scores, axis=-1, keepdims=True)
            weight = jnp.exp(scores - top)
            total = jnp.sum(weight, axis=-1, keepdims=True)
            mixed.append(matmul(weight.astype(BF16), value) * (1.0 / total))
            totals = jnp.where(lane == 2 * pair_index + which, top + jnp.log(total), totals)
        joined = jnp.where(lane < 64, mixed[0], mixed[1]).astype(BF16)
        out_ref[:, 0, :, first : first + 128] = joined.reshape(out_ref.shape[0], out_ref.shape[2], 128)
    lse_ref[0] = jnp.transpose(totals)[:8]


def attend_back_kernel(qkv_ref, bias_ref, lse_ref, grad_ref, out_ref):
    width = grad_ref.shape[-1]
    shape = (grad_ref.shape[0], grad_ref.shape[2], 128)
    rows = shape[0] * shape[1]
    bias = bias_ref[0]
    lane = lax.broadcasted_iota(jnp.int32, (rows, 128), 1)
    one = jnp.ones((rows, 128), BF16)
    for pair_index in range(width // 128):
        first = pair_index * 128
        query = qkv_ref[:, 0, :, first : first + 128].reshape(rows, 128)
        key = qkv_ref[:, 0, :, width + first : width + first + 128].reshape(rows, 128)
        value = qkv_ref[:, 0, :, 2 * width + first : 2 * width + first + 128].reshape(rows, 128)
        grad = grad_ref[:, 0, :, first : first + 128].reshape(rows, 128)
        query = (query.astype(F32) * 0.125).astype(BF16)
        query_parts, key_parts, value_parts = [], [], []
        for which in range(2):
            spot = 2 * pair_index + which
            log_total = lse_ref[0, spot : spot + 1, :]
            scores = matmul_nt(with_flag(key, bias, which), with_flag(query, one, which))
            probs = jnp.exp(scores - log_total)
            probs_grad = matmul_nt(value, half_lanes(grad, which))
            value_parts.append(matmul(probs.astype(BF16), grad))
            row_dot = jnp.sum(probs * probs_grad, axis=0, keepdims=True)
            score_grad = (probs * (probs_grad - row_dot)).astype(BF16)
            key_parts.append(matmul(score_grad, query))
            query_parts.append(matmul_tn(score_grad, key) * 0.125)
        for place, parts in enumerate((query_parts, key_parts, value_parts)):
            joined = jnp.where(lane < 64, parts[0], parts[1]).astype(BF16)
            start = place * width + first
            out_ref[:, 0, :, start : start + 128] = joined.reshape(shape)


def attention_call(kernel, arrays, outs, flops):
    def whole(array):
        shape = array.shape
        if len(shape) == 4:
            return pl.BlockSpec((shape[0], 1) + shape[2:], lambda s: (0, s, 0, 0))
        return pl.BlockSpec((1,) + shape[1:], lambda s: (s, 0, 0))

    return pl.pallas_call(
        kernel,
        grid=(arrays[0].shape[1],),
        in_specs=[whole(array) for array in arrays],
        out_specs=[whole(out) for out in outs],
        out_shape=outs,
        compiler_params=pltpu.CompilerParams(vmem_limit_bytes=40 * 1024 * 1024),
        cost_estimate=pl.CostEstimate(flops=flops, bytes_accessed=8 << 20, transcendentals=0),
    )(*arrays)


MESH = pl.DeviceIdType.MESH


def repeat(count, body):
    def step(index, carry):
        body(index)
        return carry

    lax.fori_loop(0, count, step, 0)


class Slots:
    def __init__(self):
        self.total = 0

    def take(self, count=1):
        first = self.total
        self.total += count
        return first


def layer_kernel(
    lens_ref,
    states,
    wq_own,
    vec_own,
    wo_own,
    wi_own,
    wu_own,
    encoded_out,
    o_states,
    o_wq,
    o_wout,
    o_win,
    o_wou,
    o_vecs,
    o_qkv,
    o_lse,
    o_att,
    o_norm,
    o_inv,
    o_low,
    o_act,
    o_slope,
    o_norm2,
    o_inv2,
    st_all,
    wq_all,
    vec_all,
    w_out,
    w_in,
    w_ou,
    vecs,
    qkv,
    lse,
    att,
    att_far,
    part_far,
    part_in,
    part_far2,
    part_in2,
    first_norm,
    first_inv,
    first_out,
    low2,
    act,
    slope,
    acc,
    second_inv,
    send,
    recv,
    local,
):
    d, me, y = lax.axis_index("dp"), lax.axis_index("ctx"), lax.axis_index("fsdp")
    x, c = me // 2, me % 2
    to_core = {"ctx": me + 1 - 2 * c}
    to_x = {"ctx": (me + 2) % 4}
    to_y = {"fsdp": 1 - y}
    to_z = {"dp": d + 1 - 2 * (d % 2)}
    to_zz = {"dp": (d + 2) % 4}
    to_far = {"ctx": 3 - me}
    slots = Slots()
    pending = []

    def remote(src, dst, slot, device):
        return pltpu.make_async_remote_copy(
            src_ref=src,
            dst_ref=dst,
            send_sem=send.at[slot],
            recv_sem=recv.at[slot],
            device_id=device,
            device_id_type=MESH,
        )

    def at_end(count, make):
        pending.append((count, make))

    local_slots = Slots()

    def fetch(src, dst):
        copy = pltpu.make_async_copy(src, dst, local.at[local_slots.take()])
        copy.start()
        return copy

    kept = []

    def keep(src, dst):
        kept.append(fetch(src, dst))

    barrier = pltpu.get_barrier_semaphore()
    for device in (to_core, to_x, to_y, to_z, to_zz, to_far):
        pl.semaphore_signal(barrier, inc=1, device_id=device, device_id_type=MESH)
    pl.semaphore_wait(barrier, 6)

    first = slots.take(4)
    state_x = lambda s: remote(states.at[s], st_all.at[2, s], first + s, to_x)
    second = slots.take(4)
    state_core = lambda s: remote(states.at[s], st_all.at[1, s], second + s, to_core)
    third = slots.take(4)
    state_far = lambda s: remote(st_all.at[2, s], st_all.at[3, s], third + s, to_core)
    wq_slot = slots.take()
    wq_copy = remote(wq_own, wq_all.at[pl.ds(pl.multiple_of(y * 512, 512), 512)], wq_slot, to_y)
    vec_slot = slots.take()
    vec_copy = remote(vec_own, vec_all.at[y], vec_slot, to_y)
    for s in range(4):
        state_x(s).start()
    wq_copy.start()
    vec_copy.start()
    for s in range(4):
        state_core(s).start()
    at_end(4, state_x)
    at_end(4, state_core)
    at_end(4, state_far)
    at_end(1, lambda _: wq_copy)
    at_end(1, lambda _: vec_copy)

    p = d % 2
    wo_slot = slots.take(2)

    def wo_copy(side):
        src = wo_own.at[pl.ds(pl.multiple_of(p * 256 + side * 128 + c * 64, 64), 64)]
        return remote(src, w_out.at[x if side == 0 else 1 - x, 2 * y + p], wo_slot + side, to_y)

    wo_pass_slot = slots.take(2)

    def wo_pass(side):
        here = w_out.at[x if side == 0 else 1 - x, 2 * (1 - y) + p]
        return remote(here, here, wo_pass_slot + side, to_z)

    wi_slot = slots.take(8)

    def wi_copy(b):
        src = wi_own.at[
            pl.ds(pl.multiple_of(x * 256, 256), 256), pl.ds(pl.multiple_of((2 * b + c) * 256, 256), 256)
        ]
        dst = w_in.at[
            pl.ds(pl.multiple_of(y * 512 + x * 256, 256), 256), pl.ds(pl.multiple_of(b * 256, 256), 256)
        ]
        return remote(src, dst, wi_slot + b, to_y)

    wi_pass_slot = slots.take(8)

    def wi_pass(b):
        here = w_in.at[
            pl.ds(pl.multiple_of((1 - y) * 512 + x * 256, 256), 256),
            pl.ds(pl.multiple_of(b * 256, 256), 256),
        ]
        return remote(here, here, wi_pass_slot + b, to_x)

    wu_slot = slots.take(4)

    def wu_copy(k):
        side, half = k // 2, k % 2
        src = wu_own.at[pl.ds(pl.multiple_of((p * 4 + side * 2 + c) * 256 + half * 128, 128), 128)]
        dst = w_ou.at[pl.ds(pl.multiple_of((4 * y + 2 * p + side) * 256 + half * 128, 128), 128)]
        return remote(src, dst, wu_slot + k, to_y)

    wu_pass_slot = slots.take(4)

    def wu_pass(k):
        side, half = k // 2, k % 2
        here = w_ou.at[
            pl.ds(pl.multiple_of((4 * (1 - y) + 2 * p + side) * 256 + half * 128, 128), 128)
        ]
        return remote(here, here, wu_pass_slot + k, to_z)

    for side in range(2):
        wo_copy(side).start()
    for b in range(8):
        wi_copy(b).start()
    for k in range(4):
        wu_copy(k).start()
    for count, make in ((2, wo_copy), (2, wo_pass), (8, wi_copy), (8, wi_pass), (4, wu_copy), (4, wu_pass)):
        at_end(count, make)

    own_early = [
        fetch(states, st_all.at[0]),
        fetch(wq_own, wq_all.at[pl.ds(pl.multiple_of(y * 512, 512), 512)]),
        fetch(vec_own, vec_all.at[y]),
    ]
    own_out = []
    for half in range(2):
        for side in range(2):
            src = wo_own.at[pl.ds(pl.multiple_of(half * 256 + side * 128 + c * 64, 64), 64)]
            own_out.append(fetch(src, w_out.at[x if side == 0 else 1 - x, 2 * y + half]))
    own_late = []
    for b in range(8):
        src = wi_own.at[:, pl.ds(pl.multiple_of((2 * b + c) * 256, 256), 256)]
        dst = w_in.at[pl.ds(pl.multiple_of(y * 512, 512), 512), pl.ds(b * 256, 256)]
        own_late.append(fetch(src, dst))
    for half in range(2):
        for side in range(2):
            src = wu_own.at[pl.ds(pl.multiple_of((half * 4 + side * 2 + c) * 256, 256), 256)]
            dst = w_ou.at[pl.ds(pl.multiple_of((4 * y + 2 * half + side) * 256, 256), 256)]
            own_late.append(fetch(src, dst))

    for s in range(2):
        state_x(s).wait_recv()
        state_far(s).start()
    for copy in own_early:
        copy.wait()
    vec_copy.wait_recv()
    vecs[:, :512] = vec_all[0].astype(F32)
    vecs[:, 512:] = vec_all[1].astype(F32)
    wq_copy.wait_recv()

    att_slot = slots.take(8)

    def att_copy(s, j):
        rows = pl.ds(pl.multiple_of(j * 512 + s * 128, 128), 128)
        return remote(att_far.at[j, s], att.at[rows, 256:512], att_slot + 2 * s + j, to_x)

    at_end(8, lambda k: att_copy(k // 2, k % 2))
    q_bias = jnp.concatenate((vecs[0:1, 0:128], vecs[0:1, 512:640]), 1)
    v_bias = jnp.concatenate((vecs[0:1, 128:256], vecs[0:1, 640:768]), 1)

    def key_flags(s):
        pieces = []
        for j in range(4):
            position = lax.broadcasted_iota(jnp.int32, (128, 128), 0)
            place = me + 1 - 2 * c if j == 1 else me
            place = (place + 2) % 4 if j == 2 else place
            place = 3 - me if j == 3 else place
            pieces.append(jnp.where(position + place * 128 < lens_ref[s], 0.0, MASKED))
        return jnp.concatenate(pieces, 0).astype(BF16)

    def attention(s):
        @pl.when(s < 2)
        def _():
            state_x(s + 2).wait_recv()
            state_far(s + 2).start()

        @pl.when(s == 3)
        def _():
            for side in range(2):
                wo_copy(side).wait_recv()
                wo_pass(side).start()

        state_core(s).wait_recv()
        state_far(s).wait_recv()
        rows = st_all[:, s].reshape(512, 1024)
        for place in range(3):
            made = matmul(rows, wq_all[:, place * 256 : place * 256 + 256])
            made = made + q_bias if place == 0 else made
            made = made + v_bias if place == 2 else made
            qkv[:, s, :, place * 256 : place * 256 + 256] = made.astype(BF16).reshape(4, 128, 256)
        bias = key_flags(s)
        lane = lax.broadcasted_iota(jnp.int32, (512, 128), 1)
        one = jnp.ones((512, 128), BF16)
        totals = jnp.zeros((512, 128), F32)
        for pair in range(2):
            base = pair * 128
            query = qkv[:, s, :, base : base + 128].reshape(512, 128)
            key = qkv[:, s, :, 256 + base : 384 + base].reshape(512, 128)
            value = qkv[:, s, :, 512 + base : 640 + base].reshape(512, 128)
            query = (query.astype(F32) * 0.125).astype(BF16)
            mixed = []
            for which in range(2):
                scores = matmul_nt(with_flag(query, one, which), with_flag(key, bias, which))
                top = jnp.max(scores, axis=-1, keepdims=True)
                weight = jnp.exp(scores - top)
                total = jnp.sum(weight, axis=-1, keepdims=True)
                mixed.append(matmul(weight.astype(BF16), value) * (1.0 / total))
                totals = jnp.where(lane == 2 * pair + which, top + jnp.log(total), totals)
            joined = jnp.where(lane < 64, mixed[0], mixed[1]).astype(BF16)
            for j in range(2):
                rows_j = pl.ds(pl.multiple_of(j * 512 + s * 128, 128), 128)
                att[rows_j, base : base + 128] = joined[j * 128 : j * 128 + 128]
                att_far[j, s, :, base : base + 128] = joined[256 + j * 128 : 384 + j * 128]
        for j in range(2):
            att_copy(s, j).start()
        lse[s] = jnp.transpose(totals)[:8]

    repeat(4, attention)
    for src, dst in ((st_all, o_states), (wq_all, o_wq), (vecs, o_vecs), (qkv, o_qkv), (lse, o_lse)):
        keep(src, dst)

    def pass_inner(b):
        wi_copy(b).wait_recv()
        wi_pass(b).start()

    for b in range(4):
        pass_inner(b)
    for copy in own_out:
        copy.wait()
    for side in range(2):
        wo_pass(side).wait_recv()
    for s in range(4):
        for j in range(2):
            att_copy(s, j).wait_recv()
    keep(att, o_att)
    keep(w_out, o_wout)
    out_slot = slots.take(4)

    def out_copy(n):
        return remote(part_far.at[n], part_in.at[n], out_slot + n, to_core)

    at_end(4, out_copy)
    for n in range(4):
        right = w_out[:, :, :, n * 256 : n * 256 + 256].reshape(512, 256)
        part_far[n] = matmul(att[512:], right).astype(BF16)
        out_copy(n).start()
    for b in range(4, 6):
        pass_inner(b)
    for n in range(4):
        right = w_out[:, :, :, n * 256 : n * 256 + 256].reshape(512, 256)
        made = matmul(att[:512], right) + vecs[1:2, n * 256 : n * 256 + 256]
        made = made + st_all[0, :, :, n * 256 : n * 256 + 256].astype(F32).reshape(512, 256)
        out_copy(n).wait_recv()
        first_norm[:, n * 256 : n * 256 + 256] = made + part_in[n].astype(F32)

    low_slot = slots.take(4)

    def low_copy(k):
        src = low2.at[pl.ds(pl.multiple_of(k * 128, 128), 128)]
        dst = low2.at[pl.ds(pl.multiple_of(512 + k * 128, 128), 128)]
        return remote(src, dst, low_slot + k, to_core)

    at_end(4, low_copy)

    def norm_first(k):
        for half in range(2):
            rows = pl.ds(pl.multiple_of(k * 128 + half * 64, 64), 64)
            made, normed, inverse = norm_rows(first_norm[rows, :], vecs[2:3, :], vecs[3:4, :])
            first_norm[rows, :] = normed
            first_inv[rows, :] = jnp.broadcast_to(inverse, (64, 128))
            first_out[rows, :] = made
            low2[rows, :] = made.astype(BF16)
        low_copy(k).start()

    repeat(4, norm_first)
    for b in range(6, 8):
        pass_inner(b)
    for k in range(4):
        low_copy(k).wait_recv()
    for copy in own_late:
        copy.wait()
    for src, dst in ((first_norm, o_norm), (first_inv, o_inv), (low2, o_low)):
        keep(src, dst)

    def unit_block(b):
        wi_pass(b).wait_recv()
        here = pl.ds(pl.multiple_of(b * 256, 256), 256)
        spot = pl.ds(pl.multiple_of((b // 4) * 512 + c * 256, 256), 256)
        row = vecs[pl.ds(8 + b % 4, 1), spot]
        for m in range(2):
            hidden = matmul(low2[m * 512 : m * 512 + 512, :], w_in[:, here]) + row
            below = 0.5 * (1.0 + lax.erf(hidden * math.sqrt(0.5)))
            bell = jnp.exp(-0.5 * hidden * hidden) * (1.0 / math.sqrt(2 * math.pi))
            act[m * 512 : m * 512 + 512, here] = (hidden * below).astype(BF16)
            slope[m * 512 : m * 512 + 512, here] = (below + hidden * bell).astype(BF16)

    repeat(8, unit_block)
    for src, dst in ((act, o_act), (slope, o_slope), (w_in, o_win)):
        keep(src, dst)
    mine = pl.ds(pl.multiple_of(y * 1024, 1024), 1024)
    theirs = pl.ds(pl.multiple_of((1 - y) * 1024, 1024), 1024)
    for k in range(2):
        wu_copy(k).wait_recv()
        wu_pass(k).start()

    def outer_own(n):
        here = pl.ds(pl.multiple_of(n * 256, 256), 256)
        for m in range(2):
            acc[m * 512 : m * 512 + 512, here] = matmul(
                act[m * 512 : m * 512 + 512, mine], w_ou[mine, here]
            )

    repeat(4, outer_own)
    for k in range(2, 4):
        wu_copy(k).wait_recv()
        wu_pass(k).start()
    for k in range(4):
        wu_pass(k).wait_recv()
    keep(w_ou, o_wou)
    sum_slot = slots.take(4)

    def sum_copy(n):
        return remote(part_far2.at[n], part_in2.at[n], sum_slot + n, to_core)

    at_end(4, sum_copy)

    def outer_far(n):
        here = pl.ds(pl.multiple_of(n * 256, 256), 256)
        made = acc[512:, here] + matmul(act[512:, theirs], w_ou[theirs, here])
        part_far2[n] = made.astype(BF16)
        sum_copy(n).start()

    repeat(4, outer_far)

    def outer_near(n):
        here = pl.ds(pl.multiple_of(n * 256, 256), 256)
        made = acc[:512, here] + matmul(act[:512, theirs], w_ou[theirs, here])
        made = made + first_out[:, here] + vecs[4:5, here]
        sum_copy(n).wait_recv()
        acc[:512, here] = made + part_in2[n].astype(F32)

    repeat(4, outer_near)

    def norm_second(k):
        valid_place = lax.broadcasted_iota(jnp.int32, (128, 1), 0) + me * 128
        valid = jnp.where(valid_place < lens_ref[k], 1.0, 0.0)
        for half in range(2):
            rows = pl.ds(pl.multiple_of(k * 128 + half * 64, 64), 64)
            made, normed, inverse = norm_rows(acc[rows, :], vecs[5:6, :], vecs[6:7, :])
            encoded_out[rows, :] = (made * valid[half * 64 : half * 64 + 64]).astype(BF16)
            acc[rows, :] = normed
            second_inv[rows, :] = jnp.broadcast_to(inverse, (64, 128))

    repeat(4, norm_second)
    keep(acc.at[:512], o_norm2)
    keep(second_inv, o_inv2)
    for copy in kept:
        copy.wait()
    for count, make in pending:
        for k in range(count):
            make(k).wait_send()


def layer_call(arrays):
    any_space = pl.BlockSpec(memory_space=pl.ANY)
    v = pltpu.VMEM
    return pl.pallas_call(
        layer_kernel,
        in_specs=[pl.BlockSpec(memory_space=pltpu.SMEM)] + [any_space] * 6,
        out_specs=[pl.BlockSpec(memory_space=pltpu.VMEM)] + [any_space] * 16,
        out_shape=[
            jax.ShapeDtypeStruct(shape, kind)
            for shape, kind in (
                ((512, 1024), BF16),
                ((4, 4, 128, 1024), BF16),
                ((1024, 768), BF16),
                ((2, 4, 64, 1024), BF16),
                ((1024, 2048), BF16),
                ((2048, 1024), BF16),
                ((16, 1024), F32),
                ((4, 4, 128, 768), BF16),
                ((4, 8, 512), F32),
                ((1024, 512), BF16),
                ((512, 1024), F32),
                ((512, 128), F32),
                ((1024, 1024), BF16),
                ((1024, 2048), BF16),
                ((1024, 2048), BF16),
                ((512, 1024), F32),
                ((512, 128), F32),
            )
        ],
        scratch_shapes=[
            v((4, 4, 128, 1024), BF16),
            v((1024, 768), BF16),
            v((2, 16, 512), BF16),
            v((2, 4, 64, 1024), BF16),
            v((1024, 2048), BF16),
            v((2048, 1024), BF16),
            v((16, 1024), F32),
            v((4, 4, 128, 768), BF16),
            v((4, 8, 512), F32),
            v((1024, 512), BF16),
            v((2, 4, 128, 256), BF16),
            v((4, 512, 256), BF16),
            v((4, 512, 256), BF16),
            v((4, 512, 256), BF16),
            v((4, 512, 256), BF16),
            v((512, 1024), F32),
            v((512, 128), F32),
            v((512, 1024), F32),
            v((1024, 1024), BF16),
            v((1024, 2048), BF16),
            v((1024, 2048), BF16),
            v((1024, 1024), F32),
            v((512, 128), F32),
            pltpu.SemaphoreType.DMA((80,)),
            pltpu.SemaphoreType.DMA((80,)),
            pltpu.SemaphoreType.DMA((64,)),
        ],
        compiler_params=pltpu.CompilerParams(
            collective_id=0, has_side_effects=True, vmem_limit_bytes=64 * 1024 * 1024 - 65536
        ),
    )(*arrays)


def accumulate(dst, src, lead, rows):
    steps = rows // 32
    total = math.prod(lead) * steps

    def body(index):
        place = []
        rest = index // steps
        for size in reversed(lead):
            place.insert(0, rest % size)
            rest = rest // size
        here = tuple(place) + (pl.ds(pl.multiple_of((index % steps) * 32, 32), 32),)
        dst[here] = add_low(dst[here], src[here])

    repeat(total, body)


def back_kernel(
    lens_ref,
    i_cot,
    i_n2,
    i_i2,
    i_vecs,
    i_w_ou,
    i_act,
    i_slope,
    i_low,
    i_w_in,
    i_n1,
    i_i1,
    i_att,
    i_w_out,
    i_qkv,
    i_lse,
    i_wq,
    i_states,
    grad_out,
    ou_out,
    in_out,
    out_out,
    qkv_out,
    vec_out,
    cot,
    n2,
    i2,
    vecs,
    w_ou,
    act,
    slope,
    low,
    w_in,
    n1,
    i1,
    att,
    w_out,
    qkv,
    lse,
    wq,
    outer2,
    part_in,
    branch2,
    mix_all,
    mix_far,
    g_ou,
    a_ou,
    b_ou,
    z_ou,
    zz_ou,
    a_in,
    b_in,
    z_in,
    zz_in,
    f_in,
    c_in,
    g_o,
    z_o,
    zz_o,
    x_o,
    y_o,
    g_q,
    y_q,
    z_q,
    zz_q,
    s_q,
    r_q,
    bias_q,
    vb,
    vr,
    send,
    recv,
    local,
):
    d, me, y = lax.axis_index("dp"), lax.axis_index("ctx"), lax.axis_index("fsdp")
    x, c = me // 2, me % 2
    p, q = d % 2, d // 2
    to_core = {"ctx": me + 1 - 2 * c}
    to_x = {"ctx": (me + 2) % 4}
    to_y = {"fsdp": 1 - y}
    to_z = {"dp": d + 1 - 2 * (d % 2)}
    to_zz = {"dp": (d + 2) % 4}
    to_far = {"ctx": 3 - me}
    slots = Slots()
    local_slots = Slots()
    pending = []

    def remotes(count, parts):
        first = slots.take(count)

        def make(k):
            src, dst, device = parts(k)
            return pltpu.make_async_remote_copy(
                src_ref=src,
                dst_ref=dst,
                send_sem=send.at[first + k],
                recv_sem=recv.at[first + k],
                device_id=device,
                device_id_type=MESH,
            )

        pending.append((count, make))
        return make

    def fetch(src, dst):
        copy = pltpu.make_async_copy(src, dst, local.at[local_slots.take()])
        copy.start()
        return copy

    early = [fetch(i_cot, cot), fetch(i_n2, n2), fetch(i_i2, i2), fetch(i_vecs, vecs)]
    barrier = pltpu.get_barrier_semaphore()
    for device in (to_core, to_x, to_y, to_z, to_zz, to_far):
        pl.semaphore_signal(barrier, inc=1, device_id=device, device_id_type=MESH)
    vb[0] = jnp.zeros((24, 1024), F32)
    bias_q[...] = jnp.zeros((8, 768), F32)
    for copy in early:
        copy.wait()
    got_act, got_w_ou = fetch(i_act, act), fetch(i_w_ou, w_ou)
    pl.semaphore_wait(barrier, 6)

    def chunk_of(buffer):
        def parts(k):
            src = buffer.at[pl.ds(pl.multiple_of(k * 128, 128), 128)]
            dst = buffer.at[pl.ds(pl.multiple_of(512 + k * 128, 128), 128)]
            return src, dst, to_core

        return parts

    outer_copy = remotes(4, chunk_of(outer2))
    branch_copy = remotes(4, chunk_of(branch2))

    def count_in(row, values):
        vb[0, row : row + 1, :] += jnp.sum(values, axis=0, keepdims=True)

    def norm_second(k):
        place = lax.broadcasted_iota(jnp.int32, (128, 1), 0) + me * 128
        valid = jnp.where(place < lens_ref[k], 1.0, 0.0)
        for half in range(2):
            rows = pl.ds(pl.multiple_of(k * 128 + half * 64, 64), 64)
            upstream = cot[k, half * 64 : half * 64 + 64].astype(F32) * valid[half * 64 : half * 64 + 64]
            normed = n2[rows, :]
            count_in(0, upstream * normed)
            count_in(1, upstream)
            made = norm_back(upstream, normed, i2[rows, 0:1], vecs[5:6, :])
            n2[rows, :] = made
            made = made.astype(BF16)
            outer2[rows, :] = made
            count_in(2, made.astype(F32))
        outer_copy(k).start()

    repeat(4, norm_second)
    late = [fetch(i_slope, slope), fetch(i_w_in, w_in)]
    got_act.wait()
    for k in range(4):
        outer_copy(k).wait_recv()

    def ou_first(k, x_first):
        if x_first:
            return g_ou.at[k, 1 - x], a_ou.at[k], to_x
        return g_ou.at[k, :, 1 - y], a_ou.at[k], to_y

    ou_a_x = remotes(2, lambda k: ou_first(k, True))
    ou_a_y = remotes(2, lambda k: ou_first(k + 2, False))
    ou_b_y = remotes(2, lambda k: (a_ou.at[k, 1 - y], b_ou.at[k], to_y))
    ou_b_x = remotes(2, lambda k: (a_ou.at[k + 2, 1 - x], b_ou.at[k + 2], to_x))
    ou_z = remotes(2, lambda k: (b_ou.at[2 * k + 1 - p], z_ou.at[k], to_z))
    ou_zz = remotes(1, lambda k: (z_ou.at[1 - q], zz_ou, to_zz))

    def ou_add_a(k):
        if k < 2:
            ou_a_x(k).wait_recv()
            accumulate(a_ou.at[k], g_ou.at[k, x], (2,), 128)
            ou_b_y(k).start()
        else:
            ou_a_y(k - 2).wait_recv()
            accumulate(a_ou.at[k], g_ou.at[k, :, y], (2,), 128)
            ou_b_x(k - 2).start()

    def ou_add_b(k):
        if k < 2:
            ou_b_y(k).wait_recv()
            accumulate(b_ou.at[k], a_ou.at[k, y], (), 128)
        else:
            ou_b_x(k - 2).wait_recv()
            accumulate(b_ou.at[k], a_ou.at[k, x], (), 128)

    def ou_add_z():
        for k in range(2):
            ou_z(k).wait_recv()
            accumulate(z_ou.at[k], b_ou.at[2 * k + p], (), 128)
        ou_zz(0).start()

    def ou_last():
        ou_zz(0).wait_recv()

        def body(i):
            rows = pl.ds(pl.multiple_of(i * 32, 32), 32)
            ou_out[rows, :] = z_ou[q, rows, :].astype(F32) + zz_ou[rows, :].astype(F32)

        repeat(4, body)

    in_a_x = remotes(1, lambda k: (act.at[0, 1 - x], a_in.at[0], to_x))
    in_a_y = remotes(3, lambda k: (act.at[k + 1, :, :, 1 - y], a_in.at[k + 1], to_y))
    in_b_y = remotes(1, lambda k: (a_in.at[0, :, 1 - y], b_in.at[0], to_y))
    in_b_x = remotes(3, lambda k: (a_in.at[k + 1, 1 - x], b_in.at[k + 1], to_x))
    in_z = remotes(2, lambda k: (b_in.at[2 * k + 1 - p], z_in.at[k], to_z))
    in_zz = remotes(1, lambda k: (z_in.at[1 - q], zz_in, to_zz))
    in_core = remotes(1, lambda k: (f_in.at[1 - c], c_in, to_core))

    def in_add_a(k):
        if k < 1:
            in_a_x(0).wait_recv()
            accumulate(a_in.at[0], act.at[0, x], (2, 2), 32)
            in_b_y(0).start()
        else:
            in_a_y(k - 1).wait_recv()
            accumulate(a_in.at[k], act.at[k, :, :, y], (2, 2), 32)
            in_b_x(k - 1).start()

    def in_add_b(k):
        if k < 1:
            in_b_y(0).wait_recv()
            accumulate(b_in.at[0], a_in.at[0, :, y], (2,), 32)
        else:
            in_b_x(k - 1).wait_recv()
            accumulate(b_in.at[k], a_in.at[k, x], (2,), 32)

    def in_add_z():
        for k in range(2):
            in_z(k).wait_recv()
            accumulate(z_in.at[k], b_in.at[2 * k + p], (2,), 32)
        in_zz(0).start()

    def in_sum():
        in_zz(0).wait_recv()
        for k in range(2):
            f_in[k] = z_in[q, k].astype(F32) + zz_in[k].astype(F32)
        in_core(0).start()

    def in_last():
        def place(b, own):
            return pl.ds(pl.multiple_of((2 * b + (c if own else 1 - c)) * 256, 256), 256)

        for b in range(8):
            in_out[:, place(b, True)] = f_in[c, :, b * 256 : b * 256 + 256]
        in_core(0).wait_recv()
        for b in range(8):
            in_out[:, place(b, False)] = c_in[:, b * 256 : b * 256 + 256]

    o_z = remotes(1, lambda k: (g_o.at[:, :, 1 - p], z_o, to_z))
    o_zz = remotes(1, lambda k: (z_o.at[:, 1 - q], zz_o, to_zz))
    o_x = remotes(1, lambda k: (zz_o.at[1], x_o, to_x))
    o_y = remotes(1, lambda k: (x_o.at[1 - y], y_o, to_y))

    def o_add_z():
        o_z(0).wait_recv()
        accumulate(z_o, g_o.at[:, :, p], (2, 2, 2), 32)
        o_zz(0).start()

    def o_add_zz():
        o_zz(0).wait_recv()
        accumulate(zz_o, z_o.at[:, q], (2, 2), 32)
        o_x(0).start()

    def o_add_x():
        o_x(0).wait_recv()
        accumulate(x_o, zz_o.at[0], (2,), 32)
        o_y(0).start()

    def o_last():
        o_y(0).wait_recv()
        out_out[...] = x_o[y].astype(F32) + y_o[...].astype(F32)

    q_y = remotes(4, lambda k: (g_q.at[k, :, 1 - y], y_q.at[k], to_y))
    q_z = remotes(2, lambda k: (y_q.at[2 * k + 1 - p], z_q.at[k], to_z))
    q_zz = remotes(1, lambda k: (z_q.at[1 - q], zz_q, to_zz))
    others = ((me + 1 - 2 * c, to_core), ((me + 2) % 4, to_x), (3 - me, to_far))
    q_all = [
        remotes(1, lambda k, j=j: (s_q.at[others[j][0]], r_q.at[j], others[j][1])) for j in range(3)
    ]

    def q_add_y(k):
        q_y(k).wait_recv()
        accumulate(y_q.at[k], g_q.at[k, :, y], (4,), 32)

    def q_add_z():
        for k in range(2):
            q_z(k).wait_recv()
            accumulate(z_q.at[k], y_q.at[2 * k + p], (4,), 32)
        q_zz(0).start()

    def q_sum():
        q_zz(0).wait_recv()
        for k in range(4):
            s_q[k] = z_q[q, k].astype(F32) + zz_q[k].astype(F32)
        for j in range(3):
            q_all[j](0).start()

    def q_last():
        qkv_out[me] = s_q[me]
        for j in range(3):
            q_all[j](0).wait_recv()
            qkv_out[others[j][0]] = r_q[j]

    v_core = remotes(1, lambda k: (vb.at[0, pl.ds(0, 8)], vr.at[0, pl.ds(0, 8)], to_core))
    v_x = remotes(1, lambda k: (vb.at[1, pl.ds(0, 16)], vr.at[1, pl.ds(0, 16)], to_x))
    v_y = remotes(1, lambda k: (vb.at[2], vr.at[2], to_y))
    v_z = remotes(1, lambda k: (vb.at[3], vr.at[3], to_z))
    v_zz = remotes(1, lambda k: (vb.at[4], vr.at[4], to_zz))

    def outer_grad(i):
        k = (i % 2) * 2 + i // 2
        for half in range(2):
            spot = pl.ds(pl.multiple_of((2 * k + half) * 256, 256), 256)
            left = act[:, :, :, :, :, spot].reshape(1024, 256)
            made = matmul_tn(left, outer2[...])
            g_ou[k, half] = made.astype(BF16).reshape(2, 128, 1024)

        @pl.when(i % 2 == 0)
        def _():
            ou_a_x(k).start()

        @pl.when(i % 2 == 1)
        def _():
            ou_a_y(k - 2).start()

    repeat(4, outer_grad)
    got_w_ou.wait()
    for copy in late:
        copy.wait()
    late = [fetch(i_n1, n1), fetch(i_i1, i1), fetch(i_low, low), fetch(i_att, att), fetch(i_w_out, w_out)]
    late += [fetch(i_qkv, qkv), fetch(i_lse, lse), fetch(i_wq, wq)]

    def hidden_grad(b):
        here = pl.ds(pl.multiple_of(b * 256, 256), 256)
        total = jnp.zeros((1, 256), F32)
        for m in range(2):
            made = matmul_nt(outer2[m * 512 : m * 512 + 512, :], w_ou[here, :])
            made = (made * slope[m * 512 : m * 512 + 512, here].astype(F32)).astype(BF16)
            slope[m * 512 : m * 512 + 512, here] = made
            total = total + jnp.sum(made.astype(F32), axis=0, keepdims=True)
        vb[0, pl.ds(8 + b, 1), 0:256] = total

    repeat(8, hidden_grad)

    def part_copy_parts(n):
        spot = pl.ds(pl.multiple_of(n * 256, 256), 256)
        return w_ou.at[pl.ds(1536, 512), spot], part_in.at[n], to_core

    part_copy = remotes(4, part_copy_parts)

    def first_far(n):
        here = pl.ds(pl.multiple_of(n * 256, 256), 256)
        w_ou[1536:2048, here] = matmul_nt(slope[512:, :], w_in[here, :]).astype(BF16)
        part_copy(n).start()

    repeat(4, first_far)
    ou_add_a(0)
    ou_add_a(2)

    def first_near(n):
        here = pl.ds(pl.multiple_of(n * 256, 256), 256)
        made = n2[:, here] + matmul_nt(slope[:512, :], w_in[here, :])
        part_copy(n).wait_recv()
        n2[:, here] = made + part_in[n].astype(F32)

    repeat(4, first_near)
    for copy in late:
        copy.wait()

    def norm_first(k):
        for half in range(2):
            rows = pl.ds(pl.multiple_of(k * 128 + half * 64, 64), 64)
            upstream = n2[rows, :]
            normed = n1[rows, :]
            count_in(3, upstream * normed)
            count_in(4, upstream)
            made = norm_back(upstream, normed, i1[rows, 0:1], vecs[2:3, :])
            n2[rows, :] = made
            made = made.astype(BF16)
            branch2[rows, :] = made
            count_in(5, made.astype(F32))
        branch_copy(k).start()

    repeat(4, norm_first)
    v_core(0).start()
    for k in range(4):
        branch_copy(k).wait_recv()

    mix_copy = remotes(4, lambda s: (mix_far.at[:, s], mix_all.at[pl.ds(2, 2), s], to_x))
    mix_far[...] = matmul_nt(branch2[...], w_out[1].reshape(256, 1024)).astype(BF16).reshape(2, 4, 128, 256)
    for s in range(4):
        mix_copy(s).start()
    mix_all[0:2] = matmul_nt(branch2[...], w_out[0].reshape(256, 1024)).astype(BF16).reshape(2, 4, 128, 256)

    for half in range(2):
        made = matmul_tn(att[:, half * 256 : half * 256 + 256], branch2[...])
        g_o[half] = made.astype(BF16).reshape(2, 2, 2, 32, 1024)
    o_z(0).start()
    v_core(0).wait_recv()
    vb[1, 0:8] = vb[0, 0:8] + vr[0, 0:8]
    vb[1, 8:16] = vb[0, 8:16]
    v_x(0).start()
    ou_add_a(1)
    ou_add_a(3)

    def inner_grad(k):
        left = low[:, pl.ds(pl.multiple_of(k * 256, 256), 256)]
        for half in range(4):
            made = matmul_tn(left, slope[:, half * 512 : half * 512 + 512]).astype(BF16)
            act[k, :, :, :, :, half * 512 : half * 512 + 512] = made.reshape(2, 2, 2, 32, 512)

        @pl.when(k == 0)
        def _():
            in_a_x(0).start()

        @pl.when(k > 0)
        def _():
            in_a_y(k - 1).start()

    repeat(4, inner_grad)
    got_states = []
    for j in range(4):
        for s in range(4):
            rows = pl.ds((j // 2) * 512 + s * 128, 128)
            got_states.append(fetch(i_states.at[j, s], slope.at[rows, pl.ds((j % 2) * 1024, 1024)]))

    def key_flags(s):
        pieces = []
        for j in range(4):
            position = lax.broadcasted_iota(jnp.int32, (128, 128), 0)
            place = me + 1 - 2 * c if j == 1 else me
            place = (place + 2) % 4 if j == 2 else place
            place = 3 - me if j == 3 else place
            pieces.append(jnp.where(position + place * 128 < lens_ref[s], 0.0, MASKED))
        return jnp.concatenate(pieces, 0).astype(BF16)

    hooks = {
        0: [o_add_z],
        1: [lambda: ou_add_b(0), lambda: ou_add_b(2)],
        2: [o_add_zz, lambda: ou_add_b(1), lambda: ou_z(0).start()],
        3: [lambda: ou_add_b(3), lambda: ou_z(1).start()],
    }

    def attention(s):
        for step, actions in hooks.items():

            @pl.when(s == step)
            def _():
                for action in actions:
                    action()

        mix_copy(s).wait_recv()
        bias = key_flags(s)
        lane = lax.broadcasted_iota(jnp.int32, (512, 128), 1)
        one = jnp.ones((512, 128), BF16)
        for pair in range(2):
            base = pair * 128
            query = qkv[:, s, :, base : base + 128].reshape(512, 128)
            key = qkv[:, s, :, 256 + base : 384 + base].reshape(512, 128)
            value = qkv[:, s, :, 512 + base : 640 + base].reshape(512, 128)
            grad = mix_all[:, s, :, base : base + 128].reshape(512, 128)
            query = (query.astype(F32) * 0.125).astype(BF16)
            query_parts, key_parts, value_parts = [], [], []
            for which in range(2):
                spot = 2 * pair + which
                log_total = lse[s, spot : spot + 1, :]
                scores = matmul_nt(with_flag(key, bias, which), with_flag(query, one, which))
                probs = jnp.exp(scores - log_total)
                probs_grad = matmul_nt(value, half_lanes(grad, which))
                value_parts.append(matmul(probs.astype(BF16), grad))
                row_dot = jnp.sum(probs * probs_grad, axis=0, keepdims=True)
                score_grad = (probs * (probs_grad - row_dot)).astype(BF16)
                key_parts.append(matmul(score_grad, query))
                query_parts.append(matmul_tn(score_grad, key) * 0.125)
            for place, parts in enumerate((query_parts, key_parts, value_parts)):
                joined = jnp.where(lane < 64, parts[0], parts[1]).astype(BF16)
                start = place * 256 + base
                qkv[:, s, :, start : start + 128] = joined.reshape(4, 128, 128)
                bias_q[0:1, start : start + 128] += jnp.sum(joined.astype(F32), axis=0, keepdims=True)

    repeat(4, attention)

    def piece_copy_parts(k):
        rows = pl.ds(pl.multiple_of((k % 2) * 512, 512), 512)
        spot = pl.ds(pl.multiple_of((k // 2) * 256, 256), 256)
        return w_ou.at[rows, spot], w_in.at[rows, spot], to_core

    piece_copy = remotes(8, piece_copy_parts)

    def pass_copy_parts(n):
        src = w_ou.at[pl.ds(1024, 512), pl.ds(pl.multiple_of(n * 256, 256), 256)]
        dst = w_in.at[pl.ds(0, 512), pl.ds(pl.multiple_of(1024 + n * 256, 256), 256)]
        return src, dst, to_x

    pass_copy = remotes(4, pass_copy_parts)

    def piece(j, n):
        rows = wq[pl.ds(pl.multiple_of(n * 256, 256), 256), :]
        return matmul_nt(qkv[j].reshape(512, 768), rows)

    def far_pieces(n):
        spot = pl.ds(pl.multiple_of(n * 256, 256), 256)
        w_ou[512:1024, spot] = piece(3, n).astype(BF16)
        piece_copy(2 * n + 1).start()
        w_ou[0:512, spot] = piece(1, n).astype(BF16)
        piece_copy(2 * n).start()

    repeat(4, far_pieces)

    def passed(n):
        spot = pl.ds(pl.multiple_of(n * 256, 256), 256)
        made = piece(2, n)
        piece_copy(2 * n + 1).wait_recv()
        w_ou[1024:1536, spot] = (made + w_in[512:1024, spot].astype(F32)).astype(BF16)
        pass_copy(n).start()

    repeat(4, passed)
    v_x(0).wait_recv()
    vb[2, 0:16] = vb[1, 0:16] + vr[1, 0:16]
    vb[2, 16:24] = jnp.concatenate((bias_q[...], jnp.zeros((8, 256), F32)), 1)
    v_y(0).start()
    for copy in got_states:
        copy.wait()

    def projection_grad(k):
        made = jnp.zeros((256, 768), F32)
        for j in range(4):
            spot = pl.ds(pl.multiple_of((j % 2) * 1024 + k * 256, 256), 256)
            left = slope[(j // 2) * 512 : (j // 2) * 512 + 512, spot]
            made = made + matmul_tn(left, qkv[j].reshape(512, 768))
        g_q[k] = made.astype(BF16).reshape(4, 2, 32, 768)
        q_y(k).start()

    repeat(4, projection_grad)
    in_add_a(0)
    in_add_a(1)
    v_y(0).wait_recv()
    vb[3] = vb[2] + vr[2]
    v_z(0).start()
    o_add_x()
    ou_add_z()
    in_add_a(2)
    in_add_a(3)
    v_z(0).wait_recv()
    vb[4] = vb[3] + vr[3]
    v_zz(0).start()
    in_add_b(0)
    in_add_b(1)
    in_z(0).start()

    def near_piece(n):
        spot = pl.ds(pl.multiple_of(n * 256, 256), 256)
        made = n2[:, spot] + piece(0, n)
        piece_copy(2 * n).wait_recv()
        n2[:, spot] = made + w_in[0:512, spot].astype(F32)

    repeat(4, near_piece)
    ou_last()
    o_last()
    for k in range(2):
        q_add_y(k)
    q_z(0).start()
    in_add_b(2)
    in_add_b(3)
    in_z(1).start()
    for k in range(2, 4):
        q_add_y(k)
    q_z(1).start()
    in_add_z()
    q_add_z()
    v_zz(0).wait_recv()
    vec_out[...] = vb[4] + vr[4]
    in_sum()
    q_sum()

    def last_piece(n):
        spot = pl.ds(pl.multiple_of(n * 256, 256), 256)
        far = pl.ds(pl.multiple_of(1024 + n * 256, 256), 256)
        pass_copy(n).wait_recv()
        grad_out[:, spot] = (n2[:, spot] + w_in[0:512, far].astype(F32)).astype(BF16)

    repeat(4, last_piece)
    in_last()
    q_last()
    for count, make in pending:
        for k in range(count):
            make(k).wait_send()


def back_call(arrays):
    any_space = pl.BlockSpec(memory_space=pl.ANY)
    outs = (
        ((512, 1024), BF16),
        ((128, 1024), F32),
        ((32, 4096), F32),
        ((32, 1024), F32),
        ((4, 32, 768), F32),
        ((24, 1024), F32),
    )
    scratch = (
        ((4, 128, 1024), BF16),
        ((512, 1024), F32),
        ((512, 128), F32),
        ((16, 1024), F32),
        ((2048, 1024), BF16),
        ((4, 2, 2, 2, 32, 2048), BF16),
        ((1024, 2048), BF16),
        ((1024, 1024), BF16),
        ((1024, 2048), BF16),
        ((512, 1024), F32),
        ((512, 128), F32),
        ((1024, 512), BF16),
        ((2, 4, 64, 1024), BF16),
        ((4, 4, 128, 768), BF16),
        ((4, 8, 512), F32),
        ((1024, 768), BF16),
        ((1024, 1024), BF16),
        ((4, 512, 256), BF16),
        ((1024, 1024), BF16),
        ((4, 4, 128, 256), BF16),
        ((2, 4, 128, 256), BF16),
        ((4, 2, 2, 128, 1024), BF16),
        ((4, 2, 128, 1024), BF16),
        ((4, 128, 1024), BF16),
        ((2, 128, 1024), BF16),
        ((128, 1024), BF16),
        ((4, 2, 2, 32, 2048), BF16),
        ((4, 2, 32, 2048), BF16),
        ((2, 2, 32, 2048), BF16),
        ((2, 32, 2048), BF16),
        ((2, 32, 2048), F32),
        ((32, 2048), F32),
        ((2, 2, 2, 2, 32, 1024), BF16),
        ((2, 2, 2, 32, 1024), BF16),
        ((2, 2, 32, 1024), BF16),
        ((2, 32, 1024), BF16),
        ((32, 1024), BF16),
        ((4, 4, 2, 32, 768), BF16),
        ((4, 4, 32, 768), BF16),
        ((2, 4, 32, 768), BF16),
        ((4, 32, 768), BF16),
        ((4, 32, 768), F32),
        ((3, 32, 768), F32),
        ((8, 768), F32),
        ((5, 24, 1024), F32),
        ((5, 24, 1024), F32),
    )
    return pl.pallas_call(
        back_kernel,
        in_specs=[pl.BlockSpec(memory_space=pltpu.SMEM)] + [any_space] * 17,
        out_specs=[pl.BlockSpec(memory_space=pltpu.VMEM)] * len(outs),
        out_shape=[jax.ShapeDtypeStruct(shape, kind) for shape, kind in outs],
        scratch_shapes=[pltpu.VMEM(shape, kind) for shape, kind in scratch]
        + [
            pltpu.SemaphoreType.DMA((96,)),
            pltpu.SemaphoreType.DMA((96,)),
            pltpu.SemaphoreType.DMA((48,)),
        ],
        compiler_params=pltpu.CompilerParams(
            collective_id=1, has_side_effects=True, vmem_limit_bytes=64 * 1024 * 1024 - 65536
        ),
    )(*arrays)


def shards(
    states,
    cotangent,
    lengths,
    slot_source,
    query_weight,
    query_bias,
    key_weight,
    value_weight,
    value_bias,
    output_weight,
    output_bias,
    first_gain,
    first_shift,
    inner_weight,
    inner_bias,
    outer_weight,
    outer_bias,
    final_gain,
    final_shift,
):
    seq_dev, block_len, width = states.shape
    n_dp, n_ctx, n_fsdp = (lax.axis_size(name) for name in OWNERS)
    assert (n_ctx, n_fsdp) == (4, 2)
    head_size = width // HEADS
    units = inner_weight.shape[1]
    tokens = seq_dev * block_len
    d, me, y = (lax.axis_index(name) for name in OWNERS)
    x, c = me // 2, me % 2
    own_heads = HEADS // n_ctx
    cols = own_heads * head_size
    aligned = n_dp == own_heads

    def other_half(local):
        return swap(local, "fsdp", 1)

    def ordered(own, other, axis=0):
        return jnp.where(
            y == 0, jnp.concatenate((own, other), axis), jnp.concatenate((other, own), axis)
        )

    def gathered(local, axis=0):
        return ordered(local, other_half(local), axis)

    def head_cols(matrix):
        parts = matrix.reshape(matrix.shape[:-1] + (own_heads, n_ctx, head_size))
        return pick(parts, me, parts.ndim - 2).reshape(matrix.shape[:-1] + (cols,))

    my_seqs = (d * n_fsdp + y) * seq_dev + jnp.arange(seq_dev, dtype=jnp.int32)
    seq_len = jnp.sum(jnp.where(slot_source[None, :] == my_seqs[:, None], lengths[None, :], 0), axis=1)
    places = (me ^ jnp.arange(n_ctx, dtype=jnp.int32))[:, None] * block_len + jnp.arange(
        block_len, dtype=jnp.int32
    )
    key_ok = places.reshape(1, -1) < seq_len[:, None]
    key_bias = jnp.where(key_ok, 0.0, MASKED).astype(BF16)
    key_bias = jnp.broadcast_to(key_bias[:, :, None], key_bias.shape + (128,))
    valid_rows = (places[0][None, :] < seq_len[:, None]).astype(F32).reshape(-1, 1)
    full_len = n_ctx * block_len
    score_flops = 2 * seq_dev * own_heads * full_len * full_len * 128
    block = units // (4 * n_dp)
    wq_own = jnp.concatenate((head_cols(query_weight), head_cols(key_weight), head_cols(value_weight)), 1)

    def share(own):
        return jnp.concatenate((own, swap(own, "ctx", 1)), axis=0)

    def collect(both_rows):
        return both_rows[:tokens] + swap(both_rows[tokens:].astype(BF16), "ctx", 1).astype(F32)

    if aligned:
        half_bias = lambda v: pick(v.reshape(2, n_ctx, head_size), me, 1).reshape(1, -1)
        top = jnp.concatenate((half_bias(query_bias), half_bias(value_bias), jnp.zeros((1, 256), BF16)), 1)
        rows16 = [top] + [
            v.reshape(1, -1)
            for v in (output_bias, first_gain, first_shift, outer_bias, final_gain, final_shift)
        ]
        rows16 += [jnp.zeros((1, 512), BF16), inner_bias.reshape(4, 512), jnp.zeros((4, 512), BF16)]
        vec_own = jnp.concatenate(rows16, 0)
        (
            encoded,
            flat_all,
            w_qkv,
            w_out,
            w_inner,
            w_outer,
            vecs,
            qkv,
            log_total,
            attended,
            first_norm,
            first_inverse,
            first_low,
            activated,
            slope,
            second_norm,
            second_inverse,
        ) = layer_call((seq_len, states, wq_own, vec_own, output_weight, inner_weight, outer_weight))
        input_grad, outer_weight_own, inner_weight_own, output_weight_own, qkv_sum, sums = back_call(
            (
                seq_len,
                cotangent,
                second_norm,
                second_inverse,
                vecs,
                w_outer,
                activated.reshape(4, 2, 2, 2, 32, units // 2),
                slope,
                first_low,
                w_inner,
                first_norm,
                first_inverse,
                attended,
                w_out,
                qkv,
                log_total,
                w_qkv,
                flat_all,
            )
        )
        rows = width // (8 * n_dp)
        qkv_sum = qkv_sum.reshape(n_ctx, rows, 3, own_heads, head_size)
        qkv_sum = jnp.transpose(qkv_sum, (2, 1, 3, 0, 4)).reshape(3, rows, width)
        spot = ((d * n_ctx + me) * n_fsdp + y) * rows
        token_sums = lax.dynamic_slice(sums, (0, spot), (6, rows))
        inner_bias_own = lax.dynamic_slice(sums, (8 + 2 * d + x, y * block // 2), (1, block // 2)).reshape(-1)
        own_bias = [
            lax.dynamic_slice(sums, (16, i * cols + d * head_size + y * rows), (1, rows)).reshape(-1) for i in (0, 2)
        ]
        return (
            encoded.reshape(states.shape),
            input_grad.reshape(states.shape),
            qkv_sum[0],
            own_bias[0],
            qkv_sum[1],
            qkv_sum[2],
            own_bias[1],
            output_weight_own,
            token_sums[5],
            token_sums[3],
            token_sums[4],
            inner_weight_own,
            inner_bias_own,
            outer_weight_own,
            token_sums[2],
            token_sums[0],
            token_sums[1],
        )

    def other_half(local):
        return swap(local, "fsdp", 1)

    def ordered(own, other, axis=0):
        return jnp.where(
            y == 0, jnp.concatenate((own, other), axis), jnp.concatenate((other, own), axis)
        )

    def gathered(local, axis=0):
        return ordered(local, other_half(local), axis)

    wide = (query_bias, value_bias, output_bias, first_gain, first_shift, outer_bias, final_gain, final_shift)
    packed = jnp.concatenate([v.reshape(1, -1) for v in wide] + [inner_bias.reshape(-1, width // 2)])
    other_packed = other_half(packed)
    both = jnp.where(y == 0, jnp.stack((packed, other_packed)), jnp.stack((other_packed, packed)))
    b_query, b_value, b_out, g_first, s_first, b_outer, g_final, s_final = (
        both[:, i].reshape(width).astype(F32) for i in range(8)
    )
    b_inner = both[:, 8:].reshape(2 * n_dp, 2, -1)
    b_inner = pick(b_inner, c, 1).reshape(-1).astype(F32)
    w_qkv = gathered(wq_own)
    b_qkv = jnp.concatenate((head_cols(b_query), jnp.zeros((cols,), F32), head_cols(b_value)))

    from_x = swap(states, "ctx", 2)
    from_core = swap(states, "ctx", 1)
    from_far = swap(from_x, "ctx", 1)
    flat_all = jnp.stack((states, from_core, from_x, from_far)).reshape(-1, width)

    w_out = gathered(pick(output_weight.reshape(-1, 2, 2, head_size, width), c, 2))
    w_out = jnp.concatenate((pick(w_out, x, 1), pick(w_out, 1 - x, 1)), 0).reshape(-1, width)
    w_inner = gathered(
        pick(inner_weight.reshape(width // 2, 2 * n_dp, 2, block), c, 2).reshape(width // 2, -1)
    )
    w_outer = gathered(pick(outer_weight.reshape(n_dp, 2, block, width), c, 1).reshape(-1, width))

    qkv = (matmul(flat_all, w_qkv) + b_qkv).astype(BF16)
    qkv = qkv.reshape(n_ctx, seq_dev, block_len, 3 * cols)
    attended_all, log_total = attention_call(
        attend_kernel,
        (qkv, key_bias),
        (
            jax.ShapeDtypeStruct((n_ctx, seq_dev, block_len, cols), BF16),
            jax.ShapeDtypeStruct((seq_dev, 8, full_len), F32),
        ),
        2 * score_flops,
    )
    near = attended_all[:2].reshape(-1, cols)
    far = swap(attended_all[2:], "ctx", 2).reshape(-1, cols)
    attended = jnp.concatenate((near, far), axis=1)
    first_sum = states.reshape(-1, width).astype(F32) + collect(matmul(attended, w_out)) + b_out
    first_out, first_norm, first_inverse = norm_rows(first_sum, g_first, s_first)
    first_low = share(first_out.astype(BF16))
    hidden = matmul(first_low, w_inner) + b_inner
    below = 0.5 * (1.0 + lax.erf(hidden * math.sqrt(0.5)))
    bell = jnp.exp(-0.5 * hidden * hidden) * (1.0 / math.sqrt(2 * math.pi))
    slope = (below + hidden * bell).astype(BF16)
    activated = (hidden * below).astype(BF16)
    second_sum = first_out + collect(matmul(activated, w_outer)) + b_outer
    second_out, second_norm, second_inverse = norm_rows(second_sum, g_final, s_final)
    encoded = (second_out * valid_rows).astype(BF16).reshape(states.shape)

    out_grad = cotangent.reshape(-1, width).astype(F32) * valid_rows
    final_gain_part = jnp.sum(out_grad * second_norm, axis=0)
    final_shift_part = jnp.sum(out_grad, axis=0)
    second_grad = norm_back(out_grad, second_norm, second_inverse, g_final)
    outer_round_own = second_grad.astype(BF16)
    outer_bias_part = col_sum(outer_round_own)
    outer_round = share(outer_round_own)
    outer_weight_part = matmul_tn(activated, outer_round).astype(BF16)
    hidden_grad = (matmul_nt(outer_round, w_outer) * slope.astype(F32)).astype(BF16)
    inner_bias_part = col_sum(hidden_grad)
    inner_weight_part = matmul_tn(first_low, hidden_grad).astype(BF16)
    first_grad = second_grad + collect(matmul_nt(hidden_grad, w_inner))
    first_gain_part = jnp.sum(first_grad * first_norm, axis=0)
    first_shift_part = jnp.sum(first_grad, axis=0)
    sum_grad = norm_back(first_grad, first_norm, first_inverse, g_first)
    branch_own = sum_grad.astype(BF16)
    output_bias_part = col_sum(branch_own)
    branch_grad = share(branch_own)
    output_weight_part = matmul_tn(attended, branch_grad).astype(BF16)
    attended_grad = matmul_nt(branch_grad, w_out).astype(BF16)
    near_grad = attended_grad[:, :cols]
    far_grad = swap(attended_grad[:, cols:], "ctx", 2)
    attended_grad_all = jnp.concatenate((near_grad, far_grad), 0).reshape(n_ctx, seq_dev, block_len, cols)
    (qkv_grad,) = attention_call(
        attend_back_kernel,
        (qkv, key_bias, log_total, attended_grad_all),
        (jax.ShapeDtypeStruct(qkv.shape, BF16),),
        5 * score_flops,
    )
    flat_grad = qkv_grad.reshape(-1, 3 * cols)
    bias_part = col_sum(flat_grad)
    qkv_weight_part = matmul_tn(flat_all, flat_grad).astype(BF16)
    input_part = matmul_nt(flat_grad, w_qkv).reshape(n_ctx, tokens, width)
    to_core = swap(jnp.stack((input_part[1], input_part[3])).astype(BF16), "ctx", 1)
    to_x = swap((input_part[2] + to_core[1].astype(F32)).astype(BF16), "ctx", 2)
    input_grad = sum_grad + input_part[0] + to_core[0].astype(F32) + to_x.astype(F32)
    input_grad = input_grad.astype(BF16).reshape(states.shape)

    token_sums = jnp.stack(
        (final_gain_part, final_shift_part, outer_bias_part, first_gain_part, first_shift_part, output_bias_part)
    )
    def placed_heads(part):
        whole = jnp.zeros(part.shape[:-1] + (own_heads, n_ctx, head_size), part.dtype)
        part = part.reshape(part.shape[:-1] + (own_heads, 1, head_size))
        return lax.dynamic_update_slice_in_dim(whole, part, me, part.ndim - 2).reshape(
            part.shape[:-3] + (width,)
        )

    def placed_units(part, axis):
        split = part.shape[:axis] + (2 * n_dp, 1, block) + part.shape[axis + 1 :]
        whole = jnp.zeros(split[: axis + 1] + (2,) + split[axis + 2 :], part.dtype)
        whole = lax.dynamic_update_slice_in_dim(whole, part.reshape(split), c, axis + 1)
        return whole.reshape(part.shape[:axis] + (units,) + part.shape[axis + 1 :])

    def placed_rows(part):
        part = part.reshape(2, own_heads, 1, 1, head_size, width)
        whole = jnp.zeros((own_heads, 2, 2, head_size, width), part.dtype)
        whole = lax.dynamic_update_slice(whole, part[0], (0, x, c, 0, 0))
        whole = lax.dynamic_update_slice(whole, part[1], (0, 1 - x, c, 0, 0))
        return whole.reshape(width, width)

    def owned(part):
        return lax.psum_scatter(part, OWNERS, scatter_dimension=0, tiled=True).astype(F32)

    qkv_weights = [owned(placed_heads(qkv_weight_part[:, i * cols : (i + 1) * cols])) for i in range(3)]
    query_bias_own = owned(placed_heads(bias_part[:cols]))
    value_bias_own = owned(placed_heads(bias_part[2 * cols :]))
    output_weight_own = owned(placed_rows(output_weight_part))
    inner_weight_own = owned(placed_units(inner_weight_part, 1))
    inner_bias_own = owned(placed_units(inner_bias_part, 0))
    outer_weight_own = owned(placed_units(outer_weight_part, 0))
    sums = [owned(token_sums[i]) for i in range(6)]

    return (
        encoded,
        input_grad,
        qkv_weights[0],
        query_bias_own,
        qkv_weights[1],
        qkv_weights[2],
        value_bias_own,
        output_weight_own,
        sums[5],
        sums[3],
        sums[4],
        inner_weight_own,
        inner_bias_own,
        outer_weight_own,
        sums[2],
        sums[0],
        sums[1],
    )


def solution(mesh):
    tokens = P(("dp", "fsdp"), "ctx", None)
    matrix, vector = P("fsdp", None), P("fsdp")
    own_matrix, own_vector = P(OWNERS, None), P(OWNERS)
    return jax.shard_map(
        shards,
        mesh=mesh,
        in_specs=(
            tokens,
            tokens,
            P(),
            P(),
            matrix,
            vector,
            matrix,
            matrix,
            vector,
            matrix,
            vector,
            vector,
            vector,
            matrix,
            vector,
            matrix,
            vector,
            vector,
            vector,
        ),
        out_specs=(
            tokens,
            tokens,
            own_matrix,
            own_vector,
            own_matrix,
            own_matrix,
            own_vector,
            own_matrix,
            own_vector,
            own_vector,
            own_vector,
            own_matrix,
            own_vector,
            own_matrix,
            own_vector,
            own_vector,
            own_vector,
        ),
        check_vma=False,
    )
```

profile of v0, /device:TPU:0, one launch (start us, length us, event | category | flops | bytes accessed | tf_op | source)
XLA Modules:
  0.0 277.3 jit_solution(17141083564082543283)
XLA Ops:
  0.7 0.0 copy-start
  0.7 1.4 select_reduce_fusion.lens_ref
  2.2 0.8 reshape.130
  2.9 0.8 reshape.132
  3.7 0.1 reshape.131
  3.8 0.1 reshape.133
  3.9 0.7 reshape.134
  4.6 0.7 reshape.135
  5.3 0.7 reshape.136
  6.0 0.7 reshape.137
  6.6 0.7 reshape.138
  7.3 0.7 reshape.139
  8.0 0.7 reshape.140
  8.7 1.3 concatenate.11.vec_own
  10.0 1.5 copy.60
  11.5 0.0 copy-start.1
  11.5 0.8 copy.63
  12.3 0.0 copy-done
  12.3 0.5 copy.61
  12.9 0.0 copy-done.1
  12.9 0.0 copy-start.4
  12.9 0.5 copy.62
  13.5 0.1 copy.65
  13.7 0.1 copy.64
  13.8 0.1 copy-done.4
  13.9 0.9 pad_maximum_fusion.wq_own
  14.8 99.6 %shard_map.314 = (bf16[512,1024]{1,0:T(8,128)(2,1)}, bf16[4,4,128,1024]{3,2,1,0:T(8,128)(2,1)}, bf16[1024,768]{1,0:T(8,128)(2,1)}, bf16[2,4,64,1024]{3,2,1,0:T(8...) custom-call(s32[4]{0:T(128)} %select_reduce_fusion.lens_ref, ...), custom_call_target="tpu_custom_call" | custom-call | tf_op jit(solution)/shard_map/pallas_call | solution.py:596
  114.4 150.0 %shard_map.315 = (bf16[512,1024]{1,0:T(8,128)(2,1)}, f32[128,1024]{1,0:T(8,128)}, f32[32,4096]{1,0:T(8,128)}, f32[32,1024]{1,0:T(8,128)}, f32[4,32,768]{2,1,0:T(8,128)}, /*index=5*/f32[24,1024]{1,0:T(8,128)}) custom-call(s32[4]{0:T(128)} %select_reduce_fusion.lens_ref, bf16[4,128,1024]{2,1,0:T(8,128)(2,1)} %i_cot.1, f32[512,1024]{1,0:T(8,128)} %get-tuple-element.41.i_n2, ...), custom_call_target="tpu_custom_call" | custom-call | tf_op jit(solution)/shard_map/pallas_call | solution.py:1321
  264.4 1.3 dynamic-slice_bitcast_fusion
  265.7 1.3 fusion.3
  267.0 0.8 constant_dynamic-slice_fusion
  267.8 0.5 slice_bitcast_fusion
  268.3 1.3 reshape.144
  269.6 0.0 copy-start.2
  269.6 0.2 fusion.4
  269.8 0.2 copy.68
  270.0 0.0 copy-start.3
  270.0 0.9 squeeze.36
  270.9 0.2 copy.67
  271.1 0.9 squeeze.35
  272.0 0.2 copy.66
  272.2 0.9 squeeze.34
  273.1 0.0 copy-done.2
  273.1 1.0 copy.74
  274.0 1.0 copy.75
  275.0 0.7 copy.76
  275.7 0.8 copy.77
  276.5 0.8 copy.78
  (16 shorter events, 0.1 us)
Async XLA Ops:
  0.7 11.7 %copy-start = (bf16[512,1024]{1,0:T(8,128)(2,1)S(1)}, bf16[512,1024]{1,0:T(8,128)(2,1)}, u32[]{:S(2)}) copy-start(bf16[512,1024]{1,0:T(8,128)(2,1)} %param.25) | copy-start | bytes 3145732
  11.5 1.4 copy-start.1
  12.9 1.0 copy-start.4
  269.6 3.4 %copy-start.2 = (bf16[512,1024]{1,0:T(8,128)(2,1)S(1)}, bf16[512,1024]{1,0:T(8,128)(2,1)}, u32[]{:S(2)}) copy-start(bf16[512,1024]{1,0:T(8,128)(2,1)} %get-tuple-element.40) | copy-start | bytes 3145732
  270.0 4.0 %copy-start.3 = (bf16[512,1024]{1,0:T(8,128)(2,1)S(1)}, bf16[512,1024]{1,0:T(8,128)(2,1)}, u32[]{:S(2)}) copy-start(bf16[512,1024]{1,0:T(8,128)(2,1)} %get-tuple-element.57) | copy-start | bytes 3145732
  273.1 2.0 copy-start.7
  273.1 2.6 copy-start.6
  274.0 2.4 copy-start.5
where the time goes:
time: 278 us; the launch traced here: 277 us
  Pallas kernels  250 us (90%)
  local copies, waits for them, and re-layouts  24.4 us (9%)
    pallas_call x1, Pallas kernels, back_call(): pl.pallas_call(back_kernel, in_specs=[pl.BlockSpec(memory_space=pltpu.SME...  150 us
    pallas_call x1, Pallas kernels, layer_call(): pl.pallas_call(layer_kernel, in_specs=[pl.BlockSpec(memory_space=pltpu.SM...  99.6 us
    unnamed x24, local copies, waits for them, and re-layouts  6.84 us

commit v1 on v0

--- a/solution.py
+++ b/solution.py
@@ -271,23 +271,36 @@
     state_core = lambda s: remote(states.at[s], st_all.at[1, s], second + s, to_core)
     third = slots.take(4)
     state_far = lambda s: remote(st_all.at[2, s], st_all.at[3, s], third + s, to_core)
-    wq_slot = slots.take()
-    wq_copy = remote(wq_own, wq_all.at[pl.ds(pl.multiple_of(y * 512, 512), 512)], wq_slot, to_y)
+    p = d % 2
+    wq_slot = slots.take(2)
+
+    def wq_copy(k):
+        src = wq_own.at[pl.ds(pl.multiple_of(p * 256 + k * 128, 128), 128)]
+        dst = wq_all.at[pl.ds(pl.multiple_of(y * 512 + p * 256 + k * 128, 128), 128)]
+        return remote(src, dst, wq_slot + k, to_y)
+
+    wq_pass_slot = slots.take(2)
+
+    def wq_pass(k):
+        here = wq_all.at[pl.ds(pl.multiple_of((1 - y) * 512 + p * 256 + k * 128, 128), 128)]
+        return remote(here, here, wq_pass_slot + k, to_z)
+
     vec_slot = slots.take()
     vec_copy = remote(vec_own, vec_all.at[y], vec_slot, to_y)
     for s in range(4):
         state_x(s).start()
-    wq_copy.start()
     vec_copy.start()
+    for k in range(2):
+        wq_copy(k).start()
     for s in range(4):
         state_core(s).start()
     at_end(4, state_x)
     at_end(4, state_core)
     at_end(4, state_far)
-    at_end(1, lambda _: wq_copy)
+    at_end(2, wq_copy)
+    at_end(2, wq_pass)
     at_end(1, lambda _: vec_copy)
 
-    p = d % 2
     wo_slot = slots.take(2)
 
     def wo_copy(side):
@@ -367,15 +380,23 @@
             dst = w_ou.at[pl.ds(pl.multiple_of((4 * y + 2 * half + side) * 256, 256), 256)]
             own_late.append(fetch(src, dst))
 
-    for s in range(2):
-        state_x(s).wait_recv()
-        state_far(s).start()
+    state_x(0).wait_recv()
+    state_far(0).start()
+    for k in range(2):
+        wq_copy(k).wait_recv()
+        wq_pass(k).start()
+    state_x(1).wait_recv()
+    state_far(1).start()
     for copy in own_early:
         copy.wait()
     vec_copy.wait_recv()
     vecs[:, :512] = vec_all[0].astype(F32)
     vecs[:, 512:] = vec_all[1].astype(F32)
-    wq_copy.wait_recv()
+    for side in range(2):
+        wo_copy(side).wait_recv()
+        wo_pass(side).start()
+    for k in range(2):
+        wq_pass(k).wait_recv()
 
     att_slot = slots.take(8)
 
@@ -397,17 +418,24 @@
             pieces.append(jnp.where(position + place * 128 < lens_ref[s], 0.0, MASKED))
         return jnp.concatenate(pieces, 0).astype(BF16)
 
+    def pass_inner(b):
+        wi_copy(b).wait_recv()
+        wi_pass(b).start()
+
     def attention(s):
         @pl.when(s < 2)
         def _():
             state_x(s + 2).wait_recv()
             state_far(s + 2).start()
 
+        @pl.when((s == 1) | (s == 2))
+        def _():
+            for k in range(2):
+                pass_inner(2 * (s - 1) + k)
+
         @pl.when(s == 3)
         def _():
-            for side in range(2):
-                wo_copy(side).wait_recv()
-                wo_pass(side).start()
+            pass_inner(4)
 
         state_core(s).wait_recv()
         state_far(s).wait_recv()
@@ -448,11 +476,7 @@
     for src, dst in ((st_all, o_states), (wq_all, o_wq), (vecs, o_vecs), (qkv, o_qkv), (lse, o_lse)):
         keep(src, dst)
 
-    def pass_inner(b):
-        wi_copy(b).wait_recv()
-        wi_pass(b).start()
-
-    for b in range(4):
+    for b in range(5, 7):
         pass_inner(b)
     for copy in own_out:
         copy.wait()
@@ -473,8 +497,7 @@
         right = w_out[:, :, :, n * 256 : n * 256 + 256].reshape(512, 256)
         part_far[n] = matmul(att[512:], right).astype(BF16)
         out_copy(n).start()
-    for b in range(4, 6):
-        pass_inner(b)
+    pass_inner(7)
     for n in range(4):
         right = w_out[:, :, :, n * 256 : n * 256 + 256].reshape(512, 256)
         made = matmul(att[:512], right) + vecs[1:2, n * 256 : n * 256 + 256]
@@ -502,8 +525,12 @@
         low_copy(k).start()
 
     repeat(4, norm_first)
-    for b in range(6, 8):
-        pass_inner(b)
+
+    def pass_outer(k):
+        wu_copy(k).wait_recv()
+        wu_pass(k).start()
+
+    pass_outer(0)
     for k in range(4):
         low_copy(k).wait_recv()
     for copy in own_late:
@@ -512,6 +539,10 @@
         keep(src, dst)
 
     def unit_block(b):
+        @pl.when((b == 2) | (b == 5))
+        def _():
+            pass_outer(1 + b // 4)
+
         wi_pass(b).wait_recv()
         here = pl.ds(pl.multiple_of(b * 256, 256), 256)
         spot = pl.ds(pl.multiple_of((b // 4) * 512 + c * 256, 256), 256)
@@ -528,9 +559,7 @@
         keep(src, dst)
     mine = pl.ds(pl.multiple_of(y * 1024, 1024), 1024)
     theirs = pl.ds(pl.multiple_of((1 - y) * 1024, 1024), 1024)
-    for k in range(2):
-        wu_copy(k).wait_recv()
-        wu_pass(k).start()
+    pass_outer(3)
 
     def outer_own(n):
         here = pl.ds(pl.multiple_of(n * 256, 256), 256)
@@ -540,9 +569,6 @@
             )
 
     repeat(4, outer_own)
-    for k in range(2, 4):
-        wu_copy(k).wait_recv()
-        wu_pass(k).start()
     for k in range(4):
         wu_pass(k).wait_recv()
     keep(w_ou, o_wou)
@@ -720,10 +746,18 @@
     b_ou,
     z_ou,
     zz_ou,
+    az_ou,
+    azz_ou,
+    ax_ou,
+    ay_ou,
     a_in,
     b_in,
     z_in,
     zz_in,
+    az_in,
+    azz_in,
+    ax_in,
+    ay_in,
     f_in,
     c_in,
     g_o,
@@ -826,10 +860,13 @@
     for k in range(4):
         outer_copy(k).wait_recv()
 
+    low_ou, top_ou = pl.ds(0, 256), pl.ds(256, 768)
+    low_in, top_in = pl.ds(0, 512), pl.ds(512, 1536)
+
     def ou_first(k, x_first):
         if x_first:
-            return g_ou.at[k, 1 - x], a_ou.at[k], to_x
-        return g_ou.at[k, :, 1 - y], a_ou.at[k], to_y
+            return g_ou.at[k, 1 - x, :, :, top_ou], a_ou.at[k], to_x
+        return g_ou.at[k, :, 1 - y, :, top_ou], a_ou.at[k], to_y
 
     ou_a_x = remotes(2, lambda k: ou_first(k, True))
     ou_a_y = remotes(2, lambda k: ou_first(k + 2, False))
@@ -837,15 +874,19 @@
     ou_b_x = remotes(2, lambda k: (a_ou.at[k + 2, 1 - x], b_ou.at[k + 2], to_x))
     ou_z = remotes(2, lambda k: (b_ou.at[2 * k + 1 - p], z_ou.at[k], to_z))
     ou_zz = remotes(1, lambda k: (z_ou.at[1 - q], zz_ou, to_zz))
+    low_ou_z = remotes(2, lambda k: (g_ou.at[2 * k + 1 - p, :, :, :, low_ou], az_ou.at[k], to_z))
+    low_ou_zz = remotes(1, lambda k: (az_ou.at[1 - q], azz_ou, to_zz))
+    low_ou_x = remotes(1, lambda k: (azz_ou.at[1 - x], ax_ou, to_x))
+    low_ou_y = remotes(1, lambda k: (ax_ou.at[1 - y], ay_ou, to_y))
 
     def ou_add_a(k):
         if k < 2:
             ou_a_x(k).wait_recv()
-            accumulate(a_ou.at[k], g_ou.at[k, x], (2,), 128)
+            accumulate(a_ou.at[k], g_ou.at[k, x, :, :, top_ou], (2,), 128)
             ou_b_y(k).start()
         else:
             ou_a_y(k - 2).wait_recv()
-            accumulate(a_ou.at[k], g_ou.at[k, :, y], (2,), 128)
+            accumulate(a_ou.at[k], g_ou.at[k, :, y, :, top_ou], (2,), 128)
             ou_b_x(k - 2).start()
 
     def ou_add_b(k):
@@ -862,40 +903,51 @@
             accumulate(z_ou.at[k], b_ou.at[2 * k + p], (), 128)
         ou_zz(0).start()
 
+    def low_ou_add_z():
+        for k in range(2):
+            low_ou_z(k).wait_recv()
+            accumulate(az_ou.at[k], g_ou.at[2 * k + p, :, :, :, low_ou], (2, 2), 128)
+        low_ou_zz(0).start()
+
+    def low_ou_add_zz():
+        low_ou_zz(0).wait_recv()
+        accumulate(azz_ou, az_ou.at[q], (2, 2), 128)
+        low_ou_x(0).start()
+
+    def low_ou_add_x():
+        low_ou_x(0).wait_recv()
+        accumulate(ax_ou, azz_ou.at[x], (2,), 128)
+        low_ou_y(0).start()
+
     def ou_last():
         ou_zz(0).wait_recv()
+        low_ou_y(0).wait_recv()
 
         def body(i):
             rows = pl.ds(pl.multiple_of(i * 32, 32), 32)
-            ou_out[rows, :] = z_ou[q, rows, :].astype(F32) + zz_ou[rows, :].astype(F32)
+            ou_out[rows, 256:] = z_ou[q, rows, :].astype(F32) + zz_ou[rows, :].astype(F32)
+            ou_out[rows, :256] = ax_ou[y, rows, :].astype(F32) + ay_ou[rows, :].astype(F32)
 
         repeat(4, body)
 
-    in_a_x = remotes(1, lambda k: (act.at[0, 1 - x], a_in.at[0], to_x))
-    in_a_y = remotes(3, lambda k: (act.at[k + 1, :, :, 1 - y], a_in.at[k + 1], to_y))
-    in_b_y = remotes(1, lambda k: (a_in.at[0, :, 1 - y], b_in.at[0], to_y))
-    in_b_x = remotes(3, lambda k: (a_in.at[k + 1, 1 - x], b_in.at[k + 1], to_x))
+    in_a = remotes(4, lambda k: (act.at[k, :, :, 1 - y, :, top_in], a_in.at[k], to_y))
+    in_b = remotes(4, lambda k: (a_in.at[k, 1 - x], b_in.at[k], to_x))
     in_z = remotes(2, lambda k: (b_in.at[2 * k + 1 - p], z_in.at[k], to_z))
     in_zz = remotes(1, lambda k: (z_in.at[1 - q], zz_in, to_zz))
     in_core = remotes(1, lambda k: (f_in.at[1 - c], c_in, to_core))
+    low_in_z = remotes(2, lambda k: (act.at[2 * k + 1 - p, :, :, :, :, low_in], az_in.at[k], to_z))
+    low_in_zz = remotes(1, lambda k: (az_in.at[1 - q], azz_in, to_zz))
+    low_in_x = remotes(1, lambda k: (azz_in.at[1 - x], ax_in, to_x))
+    low_in_y = remotes(1, lambda k: (ax_in.at[:, 1 - y], ay_in, to_y))
 
     def in_add_a(k):
-        if k < 1:
-            in_a_x(0).wait_recv()
-            accumulate(a_in.at[0], act.at[0, x], (2, 2), 32)
-            in_b_y(0).start()
-        else:
-            in_a_y(k - 1).wait_recv()
-            accumulate(a_in.at[k], act.at[k, :, :, y], (2, 2), 32)
-            in_b_x(k - 1).start()
+        in_a(k).wait_recv()
+        accumulate(a_in.at[k], act.at[k, :, :, y, :, top_in], (2, 2), 32)
+        in_b(k).start()
 
     def in_add_b(k):
-        if k < 1:
-            in_b_y(0).wait_recv()
-            accumulate(b_in.at[0], a_in.at[0, :, y], (2,), 32)
-        else:
-            in_b_x(k - 1).wait_recv()
-            accumulate(b_in.at[k], a_in.at[k, x], (2,), 32)
+        in_b(k).wait_recv()
+        accumulate(b_in.at[k], a_in.at[k, x], (2,), 32)
 
     def in_add_z():
         for k in range(2):
@@ -903,10 +955,28 @@
             accumulate(z_in.at[k], b_in.at[2 * k + p], (2,), 32)
         in_zz(0).start()
 
+    def low_in_add_z():
+        for k in range(2):
+            low_in_z(k).wait_recv()
+            accumulate(az_in.at[k], act.at[2 * k + p, :, :, :, :, low_in], (2, 2, 2), 32)
+        low_in_zz(0).start()
+
+    def low_in_add_zz():
+        low_in_zz(0).wait_recv()
+        accumulate(azz_in, az_in.at[q], (2, 2, 2), 32)
+        low_in_x(0).start()
+
+    def low_in_add_x():
+        low_in_x(0).wait_recv()
+        accumulate(ax_in, azz_in.at[x], (2, 2), 32)
+        low_in_y(0).start()
+
     def in_sum():
         in_zz(0).wait_recv()
+        low_in_y(0).wait_recv()
         for k in range(2):
-            f_in[k] = z_in[q, k].astype(F32) + zz_in[k].astype(F32)
+            f_in[k, :, 512:] = z_in[q, k].astype(F32) + zz_in[k].astype(F32)
+            f_in[k, :, :512] = ax_in[k, y].astype(F32) + ay_in[k].astype(F32)
         in_core(0).start()
 
     def in_last():
@@ -995,6 +1065,10 @@
         @pl.when(i % 2 == 1)
         def _():
             ou_a_y(k - 2).start()
+
+        @pl.when(i >= 2)
+        def _():
+            low_ou_z(i - 2).start()
 
     repeat(4, outer_grad)
     got_w_ou.wait()
@@ -1029,6 +1103,7 @@
     repeat(4, first_far)
     ou_add_a(0)
     ou_add_a(2)
+    low_ou_add_z()
 
     def first_near(n):
         here = pl.ds(pl.multiple_of(n * 256, 256), 256)
@@ -1056,6 +1131,8 @@
 
     repeat(4, norm_first)
     v_core(0).start()
+    ou_add_a(1)
+    ou_add_a(3)
     for k in range(4):
         branch_copy(k).wait_recv()
 
@@ -1073,8 +1150,6 @@
     vb[1, 0:8] = vb[0, 0:8] + vr[0, 0:8]
     vb[1, 8:16] = vb[0, 8:16]
     v_x(0).start()
-    ou_add_a(1)
-    ou_add_a(3)
 
     def inner_grad(k):
         left = low[:, pl.ds(pl.multiple_of(k * 256, 256), 256)]
@@ -1082,13 +1157,11 @@
             made = matmul_tn(left, slope[:, half * 512 : half * 512 + 512]).astype(BF16)
             act[k, :, :, :, :, half * 512 : half * 512 + 512] = made.reshape(2, 2, 2, 32, 512)
 
-        @pl.when(k == 0)
+        in_a(k).start()
+
+        @pl.when(k % 2 == 1)
         def _():
-            in_a_x(0).start()
-
-        @pl.when(k > 0)
-        def _():
-            in_a_y(k - 1).start()
+            low_in_z(k // 2).start()
 
     repeat(4, inner_grad)
     got_states = []
@@ -1107,11 +1180,39 @@
             pieces.append(jnp.where(position + place * 128 < lens_ref[s], 0.0, MASKED))
         return jnp.concatenate(pieces, 0).astype(BF16)
 
+    def piece_copy_parts(k):
+        rows = pl.ds(pl.multiple_of((k % 2) * 512 + (k // 2) * 128, 128), 128)
+        return w_ou.at[rows], w_in.at[rows, pl.ds(0, 1024)], to_core
+
+    piece_copy = remotes(8, piece_copy_parts)
+
+    def pass_copy_parts(s):
+        src = w_ou.at[pl.ds(pl.multiple_of(1024 + s * 128, 128), 128)]
+        dst = w_in.at[pl.ds(pl.multiple_of(s * 128, 128), 128), pl.ds(1024, 1024)]
+        return src, dst, to_x
+
+    pass_copy = remotes(4, pass_copy_parts)
+
+    def far_pieces(s):
+        for which in range(2):
+            rows = pl.ds(pl.multiple_of(512 * which + s * 128, 128), 128)
+            w_ou[rows, :] = matmul_nt(qkv[1 + 2 * which, s], wq[...]).astype(BF16)
+        for which in range(2):
+            piece_copy(2 * s + which).start()
+
+    def passed(s):
+        made = matmul_nt(qkv[2, s], wq[...])
+        piece_copy(2 * s + 1).wait_recv()
+        rows = pl.ds(pl.multiple_of(512 + s * 128, 128), 128)
+        made = made + w_in[rows, 0:1024].astype(F32)
+        w_ou[pl.ds(pl.multiple_of(1024 + s * 128, 128), 128), :] = made.astype(BF16)
+        pass_copy(s).start()
+
     hooks = {
-        0: [o_add_z],
-        1: [lambda: ou_add_b(0), lambda: ou_add_b(2)],
-        2: [o_add_zz, lambda: ou_add_b(1), lambda: ou_z(0).start()],
-        3: [lambda: ou_add_b(3), lambda: ou_z(1).start()],
+        0: [lambda: ou_add_b(0), lambda: ou_add_b(2), low_ou_add_zz],
+        1: [lambda: ou_add_b(1), lambda: ou_add_b(3), lambda: ou_z(0).start(), lambda: ou_z(1).start(), o_add_z],
+        2: [lambda: in_add_a(0)],
+        3: [lambda: in_add_a(1)],
     }
 
     def attention(s):
@@ -1150,44 +1251,15 @@
                 start = place * 256 + base
                 qkv[:, s, :, start : start + 128] = joined.reshape(4, 128, 128)
                 bias_q[0:1, start : start + 128] += jnp.sum(joined.astype(F32), axis=0, keepdims=True)
+        far_pieces(s)
+
+        @pl.when(s > 0)
+        def _():
+            passed(s - 1)
 
     repeat(4, attention)
-
-    def piece_copy_parts(k):
-        rows = pl.ds(pl.multiple_of((k % 2) * 512, 512), 512)
-        spot = pl.ds(pl.multiple_of((k // 2) * 256, 256), 256)
-        return w_ou.at[rows, spot], w_in.at[rows, spot], to_core
-
-    piece_copy = remotes(8, piece_copy_parts)
-
-    def pass_copy_parts(n):
-        src = w_ou.at[pl.ds(1024, 512), pl.ds(pl.multiple_of(n * 256, 256), 256)]
-        dst = w_in.at[pl.ds(0, 512), pl.ds(pl.multiple_of(1024 + n * 256, 256), 256)]
-        return src, dst, to_x
-
-    pass_copy = remotes(4, pass_copy_parts)
-
-    def piece(j, n):
-        rows = wq[pl.ds(pl.multiple_of(n * 256, 256), 256), :]
-        return matmul_nt(qkv[j].reshape(512, 768), rows)
-
-    def far_pieces(n):
-        spot = pl.ds(pl.multiple_of(n * 256, 256), 256)
-        w_ou[512:1024, spot] = piece(3, n).astype(BF16)
-        piece_copy(2 * n + 1).start()
-        w_ou[0:512, spot] = piece(1, n).astype(BF16)
-        piece_copy(2 * n).start()
-
-    repeat(4, far_pieces)
-
-    def passed(n):
-        spot = pl.ds(pl.multiple_of(n * 256, 256), 256)
-        made = piece(2, n)
-        piece_copy(2 * n + 1).wait_recv()
-        w_ou[1024:1536, spot] = (made + w_in[512:1024, spot].astype(F32)).astype(BF16)
-        pass_copy(n).start()
-
-    repeat(4, passed)
+    passed(3)
+
     v_x(0).wait_recv()
     vb[2, 0:16] = vb[1, 0:16] + vr[1, 0:16]
     vb[2, 16:24] = jnp.concatenate((bias_q[...], jnp.zeros((8, 256), F32)), 1)
@@ -1205,56 +1277,58 @@
         q_y(k).start()
 
     repeat(4, projection_grad)
-    in_add_a(0)
-    in_add_a(1)
+    in_add_a(2)
+    low_in_add_z()
+    ou_add_z()
     v_y(0).wait_recv()
     vb[3] = vb[2] + vr[2]
     v_z(0).start()
-    o_add_x()
-    ou_add_z()
-    in_add_a(2)
+    o_add_zz()
     in_add_a(3)
+    for k in range(2):
+        in_add_b(k)
+    in_z(0).start()
+
+    def near_piece(s):
+        rows = pl.ds(pl.multiple_of(s * 128, 128), 128)
+        made = n2[rows, :] + matmul_nt(qkv[0, s], wq[...])
+        piece_copy(2 * s).wait_recv()
+        n2[rows, :] = made + w_in[rows, 0:1024].astype(F32)
+
+    repeat(4, near_piece)
+    low_ou_add_x()
+    for k in range(2):
+        q_add_y(k)
+    q_z(0).start()
+    low_in_add_zz()
+    for k in range(2, 4):
+        q_add_y(k)
+    q_z(1).start()
     v_z(0).wait_recv()
     vb[4] = vb[3] + vr[3]
     v_zz(0).start()
-    in_add_b(0)
-    in_add_b(1)
-    in_z(0).start()
-
-    def near_piece(n):
-        spot = pl.ds(pl.multiple_of(n * 256, 256), 256)
-        made = n2[:, spot] + piece(0, n)
-        piece_copy(2 * n).wait_recv()
-        n2[:, spot] = made + w_in[0:512, spot].astype(F32)
-
-    repeat(4, near_piece)
+    for k in range(2, 4):
+        in_add_b(k)
+    in_z(1).start()
+    q_add_z()
+    o_add_x()
+    low_in_add_x()
+    in_add_z()
+
+    def last_piece(s):
+        rows = pl.ds(pl.multiple_of(s * 128, 128), 128)
+        pass_copy(s).wait_recv()
+        grad_out[rows, :] = (n2[rows, :] + w_in[rows, 1024:2048].astype(F32)).astype(BF16)
+
+    repeat(4, last_piece)
     ou_last()
     o_last()
-    for k in range(2):
-        q_add_y(k)
-    q_z(0).start()
-    in_add_b(2)
-    in_add_b(3)
-    in_z(1).start()
-    for k in range(2, 4):
-        q_add_y(k)
-    q_z(1).start()
-    in_add_z()
-    q_add_z()
     v_zz(0).wait_recv()
     vec_out[...] = vb[4] + vr[4]
+    q_sum()
     in_sum()
-    q_sum()
-
-    def last_piece(n):
-        spot = pl.ds(pl.multiple_of(n * 256, 256), 256)
-        far = pl.ds(pl.multiple_of(1024 + n * 256, 256), 256)
-        pass_copy(n).wait_recv()
-        grad_out[:, spot] = (n2[:, spot] + w_in[0:512, far].astype(F32)).astype(BF16)
-
-    repeat(4, last_piece)
+    q_last()
     in_last()
-    q_last()
     for count, make in pending:
         for k in range(count):
             make(k).wait_send()
@@ -1293,14 +1367,22 @@
         ((4, 4, 128, 256), BF16),
         ((2, 4, 128, 256), BF16),
         ((4, 2, 2, 128, 1024), BF16),
-        ((4, 2, 128, 1024), BF16),
-        ((4, 128, 1024), BF16),
-        ((2, 128, 1024), BF16),
-        ((128, 1024), BF16),
-        ((4, 2, 2, 32, 2048), BF16),
-        ((4, 2, 32, 2048), BF16),
-        ((2, 2, 32, 2048), BF16),
-        ((2, 32, 2048), BF16),
+        ((4, 2, 128, 768), BF16),
+        ((4, 128, 768), BF16),
+        ((2, 128, 768), BF16),
+        ((128, 768), BF16),
+        ((2, 2, 2, 128, 256), BF16),
+        ((2, 2, 128, 256), BF16),
+        ((2, 128, 256), BF16),
+        ((128, 256), BF16),
+        ((4, 2, 2, 32, 1536), BF16),
+        ((4, 2, 32, 1536), BF16),
+        ((2, 2, 32, 1536), BF16),
+        ((2, 32, 1536), BF16),
+        ((2, 2, 2, 2, 32, 512), BF16),
+        ((2, 2, 2, 32, 512), BF16),
+        ((2, 2, 32, 512), BF16),
+        ((2, 32, 512), BF16),
         ((2, 32, 2048), F32),
         ((32, 2048), F32),
         ((2, 2, 2, 2, 32, 1024), BF16),

time: 278 us -> 252 us (0.906)
  Pallas kernels: 250 us -> 224 us
    pallas_call x1, Pallas kernels: 150 us -> 127 us  [back_call(): pl.pallas_call(back_kernel, in_specs=[pl.BlockSpec(memory_space=pltpu.SME...]
    pallas_call x1, Pallas kernels: 99.6 us -> 96.1 us  [layer_call(): pl.pallas_call(layer_kernel, in_specs=[pl.BlockSpec(memory_space=pltpu.SM...]
where the time goes in v1:
time: 252 us; the launch traced here: 251 us
  Pallas kernels  224 us (89%)
  local copies, waits for them, and re-layouts  24.4 us (10%)
    pallas_call x1, Pallas kernels, back_call(): pl.pallas_call(back_kernel, in_specs=[pl.BlockSpec(memory_space=pltpu.SME...  127 us
    pallas_call x1, Pallas kernels, layer_call(): pl.pallas_call(layer_kernel, in_specs=[pl.BlockSpec(memory_space=pltpu.SM...  96.1 us
    unnamed x24, local copies, waits for them, and re-layouts  6.84 us

profile of v1, /device:TPU:0, one launch (start us, length us, event | category | flops | bytes accessed | tf_op | source)
XLA Modules:
  0.0 251.1 jit_solution(18102545983428867196)
XLA Ops:
  0.7 0.0 copy-start
  0.7 1.4 select_reduce_fusion.lens_ref
  2.2 0.8 reshape.130
  2.9 0.8 reshape.132
  3.7 0.1 reshape.131
  3.8 0.1 reshape.133
  3.9 0.7 reshape.134
  4.6 0.7 reshape.135
  5.3 0.7 reshape.136
  6.0 0.7 reshape.137
  6.6 0.7 reshape.138
  7.3 0.7 reshape.139
  8.0 0.7 reshape.140
  8.7 1.3 concatenate.11.vec_own
  10.0 1.5 copy.60
  11.5 0.0 copy-start.1
  11.5 0.8 copy.63
  12.3 0.5 copy.61
  12.9 0.0 copy-start.4
  12.9 0.5 copy.62
  13.5 0.1 copy.65
  13.7 0.1 copy.64
  13.8 0.1 copy-done.4
  13.9 0.9 pad_maximum_fusion.wq_own
  14.8 96.1 %shard_map.314 = (bf16[512,1024]{1,0:T(8,128)(2,1)}, bf16[4,4,128,1024]{3,2,1,0:T(8,128)(2,1)}, bf16[1024,768]{1,0:T(8,128)(2,1)}, bf16[2,4,64,1024]{3,2,1,0:T(8...) custom-call(s32[4]{0:T(128)} %select_reduce_fusion.lens_ref, ...), custom_call_target="tpu_custom_call" | custom-call | tf_op jit(solution)/shard_map/pallas_call | solution.py:622
  110.9 127.4 %shard_map.315 = (bf16[512,1024]{1,0:T(8,128)(2,1)}, f32[128,1024]{1,0:T(8,128)}, f32[32,4096]{1,0:T(8,128)}, f32[32,1024]{1,0:T(8,128)}, f32[4,32,768]{2,1,0:T(8,128)}, /*index=5*/f32[24,1024]{1,0:T(8,128)}) custom-call(s32[4]{0:T(128)} %select_reduce_fusion.lens_ref, bf16[4,128,1024]{2,1,0:T(8,128)(2,1)} %i_cot.1, f32[512,1024]{1,0:T(8,128)} %get-tuple-element.41.i_n2, ...), custom_call_target="tpu_custom_call" | custom-call | tf_op jit(solution)/shard_map/pallas_call | solution.py:1403
  238.3 1.3 dynamic-slice_bitcast_fusion
  239.6 1.3 fusion.3
  240.9 0.8 constant_dynamic-slice_fusion
  241.6 0.5 slice_bitcast_fusion
  242.2 1.3 reshape.144
  243.5 0.2 fusion.4
  243.7 0.2 copy.68
  243.9 0.0 copy-start.3
  243.9 0.9 squeeze.36
  244.8 0.2 copy.67
  245.0 0.9 squeeze.35
  245.9 0.2 copy.66
  246.0 0.9 squeeze.34
  246.9 1.0 copy.74
  247.9 0.0 copy-done.3
  247.9 1.0 copy.75
  248.9 0.0 copy-done.7
  248.9 0.7 copy.76
  249.6 0.0 copy-done.6
  249.6 0.8 copy.77
  250.3 0.0 copy-done.5
  250.3 0.8 copy.78
  (16 shorter events, 0.1 us)
Async XLA Ops:
  0.7 11.7 %copy-start = (bf16[512,1024]{1,0:T(8,128)(2,1)S(1)}, bf16[512,1024]{1,0:T(8,128)(2,1)}, u32[]{:S(2)}) copy-start(bf16[512,1024]{1,0:T(8,128)(2,1)} %param.25) | copy-start | bytes 3145732
  11.5 1.4 copy-start.1
  12.9 1.0 copy-start.4
  243.5 3.4 %copy-start.2 = (bf16[512,1024]{1,0:T(8,128)(2,1)S(1)}, bf16[512,1024]{1,0:T(8,128)(2,1)}, u32[]{:S(2)}) copy-start(bf16[512,1024]{1,0:T(8,128)(2,1)} %get-tuple-element.40) | copy-start | bytes 3145732
  243.9 4.0 %copy-start.3 = (bf16[512,1024]{1,0:T(8,128)(2,1)S(1)}, bf16[512,1024]{1,0:T(8,128)(2,1)}, u32[]{:S(2)}) copy-start(bf16[512,1024]{1,0:T(8,128)(2,1)} %get-tuple-element.57) | copy-start | bytes 3145732
  246.9 2.0 copy-start.7
  246.9 2.6 %copy-start.6 = (f32[32,4096]{1,0:T(8,128)S(1)}, f32[32,4096]{1,0:T(8,128)}, u32[]{:S(2)}) copy-start(f32[32,4096]{1,0:T(8,128)} %get-tuple-element.106) | copy-start | bytes 1572868
  247.9 2.4 copy-start.5

commit v2 on v1

--- a/solution.py
+++ b/solution.py
@@ -172,11 +172,32 @@
         return first
 
 
+def read_lengths(slot_ref, length_ref, lens_ref, first):
+    def step(t, totals):
+        source, count = slot_ref[t], length_ref[t]
+        return tuple(total + jnp.where(source == first + i, count, 0) for i, total in enumerate(totals))
+
+    totals = lax.fori_loop(0, slot_ref.shape[0], step, (jnp.int32(0),) * 4)
+    for i in range(4):
+        lens_ref[i] = totals[i]
+
+
 def layer_kernel(
-    lens_ref,
+    length_ref,
+    slot_ref,
     states,
-    wq_own,
-    vec_own,
+    query_own,
+    key_own,
+    value_own,
+    vec_query,
+    vec_out,
+    vec_gain,
+    vec_shift,
+    vec_outer,
+    vec_gain2,
+    vec_shift2,
+    vec_value,
+    vec_inner,
     wo_own,
     wi_own,
     wu_own,
@@ -197,6 +218,7 @@
     o_slope,
     o_norm2,
     o_inv2,
+    lens_ref,
     st_all,
     wq_all,
     vec_all,
@@ -220,6 +242,8 @@
     slope,
     acc,
     second_inv,
+    chosen,
+    own_three,
     send,
     recv,
     local,
@@ -260,9 +284,18 @@
     def keep(src, dst):
         kept.append(fetch(src, dst))
 
+    three = [fetch(src, own_three.at[i]) for i, src in enumerate((query_own, key_own, value_own))]
     barrier = pltpu.get_barrier_semaphore()
     for device in (to_core, to_x, to_y, to_z, to_zz, to_far):
         pl.semaphore_signal(barrier, inc=1, device_id=device, device_id_type=MESH)
+    row = lax.broadcasted_iota(jnp.int32, (1024, 256), 0)
+    col = lax.broadcasted_iota(jnp.int32, (1024, 256), 1)
+    chosen[...] = jnp.where(row == (col // 64) * 256 + me * 64 + col % 64, 1.0, 0.0).astype(BF16)
+    read_lengths(slot_ref, length_ref, lens_ref, (2 * d + y) * 4)
+    singles = (vec_query, vec_out, vec_gain, vec_shift, vec_outer, vec_gain2, vec_shift2, vec_value)
+    vec_all[y, 0:8] = jnp.concatenate([single[...].astype(F32).reshape(1, 512) for single in singles], 0)
+    inner_rows = vec_inner[...].astype(F32).reshape(4, 512)
+    vec_all[y, 8:16] = jnp.concatenate((inner_rows, jnp.zeros((4, 512), F32)), 0)
     pl.semaphore_wait(barrier, 6)
 
     first = slots.take(4)
@@ -275,9 +308,8 @@
     wq_slot = slots.take(2)
 
     def wq_copy(k):
-        src = wq_own.at[pl.ds(pl.multiple_of(p * 256 + k * 128, 128), 128)]
-        dst = wq_all.at[pl.ds(pl.multiple_of(y * 512 + p * 256 + k * 128, 128), 128)]
-        return remote(src, dst, wq_slot + k, to_y)
+        here = wq_all.at[pl.ds(pl.multiple_of(y * 512 + p * 256 + k * 128, 128), 128)]
+        return remote(here, here, wq_slot + k, to_y)
 
     wq_pass_slot = slots.take(2)
 
@@ -286,12 +318,10 @@
         return remote(here, here, wq_pass_slot + k, to_z)
 
     vec_slot = slots.take()
-    vec_copy = remote(vec_own, vec_all.at[y], vec_slot, to_y)
+    vec_copy = remote(vec_all.at[y], vec_all.at[y], vec_slot, to_y)
     for s in range(4):
         state_x(s).start()
     vec_copy.start()
-    for k in range(2):
-        wq_copy(k).start()
     for s in range(4):
         state_core(s).start()
     at_end(4, state_x)
@@ -352,6 +382,12 @@
 
     for side in range(2):
         wo_copy(side).start()
+    for place in range(3):
+        three[place].wait()
+        made = matmul(own_three[place], chosen[...]).astype(BF16)
+        wq_all[pl.ds(pl.multiple_of(y * 512, 512), 512), place * 256 : place * 256 + 256] = made
+    for k in range(2):
+        wq_copy(k).start()
     for b in range(8):
         wi_copy(b).start()
     for k in range(4):
@@ -361,8 +397,6 @@
 
     own_early = [
         fetch(states, st_all.at[0]),
-        fetch(wq_own, wq_all.at[pl.ds(pl.multiple_of(y * 512, 512), 512)]),
-        fetch(vec_own, vec_all.at[y]),
     ]
     own_out = []
     for half in range(2):
@@ -390,8 +424,8 @@
     for copy in own_early:
         copy.wait()
     vec_copy.wait_recv()
-    vecs[:, :512] = vec_all[0].astype(F32)
-    vecs[:, 512:] = vec_all[1].astype(F32)
+    vecs[:, :512] = vec_all[0]
+    vecs[:, 512:] = vec_all[1]
     for side in range(2):
         wo_copy(side).wait_recv()
         wo_pass(side).start()
@@ -405,8 +439,8 @@
         return remote(att_far.at[j, s], att.at[rows, 256:512], att_slot + 2 * s + j, to_x)
 
     at_end(8, lambda k: att_copy(k // 2, k % 2))
-    q_bias = jnp.concatenate((vecs[0:1, 0:128], vecs[0:1, 512:640]), 1)
-    v_bias = jnp.concatenate((vecs[0:1, 128:256], vecs[0:1, 640:768]), 1)
+    biases = matmul(vecs[0:8, :].astype(BF16), chosen[...])
+    q_bias, v_bias = biases[0:1], biases[7:8]
 
     def key_flags(s):
         pieces = []
@@ -621,8 +655,11 @@
     v = pltpu.VMEM
     return pl.pallas_call(
         layer_kernel,
-        in_specs=[pl.BlockSpec(memory_space=pltpu.SMEM)] + [any_space] * 6,
-        out_specs=[pl.BlockSpec(memory_space=pltpu.VMEM)] + [any_space] * 16,
+        in_specs=[pl.BlockSpec(memory_space=pltpu.SMEM)] * 2
+        + [any_space] * 4
+        + [pl.BlockSpec(memory_space=pltpu.VMEM)] * 9
+        + [any_space] * 3,
+        out_specs=[pl.BlockSpec(memory_space=pltpu.VMEM)] + [any_space] * 16 + [pl.BlockSpec(memory_space=pltpu.SMEM)],
         out_shape=[
             jax.ShapeDtypeStruct(shape, kind)
             for shape, kind in (
@@ -643,12 +680,13 @@
                 ((1024, 2048), BF16),
                 ((512, 1024), F32),
                 ((512, 128), F32),
+                ((4,), jnp.int32),
             )
         ],
         scratch_shapes=[
             v((4, 4, 128, 1024), BF16),
             v((1024, 768), BF16),
-            v((2, 16, 512), BF16),
+            v((2, 16, 512), F32),
             v((2, 4, 64, 1024), BF16),
             v((1024, 2048), BF16),
             v((2048, 1024), BF16),
@@ -669,6 +707,8 @@
             v((1024, 2048), BF16),
             v((1024, 1024), F32),
             v((512, 128), F32),
+            v((1024, 256), BF16),
+            v((3, 512, 1024), BF16),
             pltpu.SemaphoreType.DMA((80,)),
             pltpu.SemaphoreType.DMA((80,)),
             pltpu.SemaphoreType.DMA((64,)),
@@ -1417,6 +1457,57 @@
     )(*arrays)
 
 
+def finish_kernel(sums_ref, qkv_ref, *refs):
+    count = 5
+    sources, targets = refs[:count], refs[count : 2 * count]
+    rows_out, inner_out, query_out, value_out = refs[2 * count : 2 * count + 6], *refs[2 * count + 6 : 2 * count + 9]
+    projections = refs[2 * count + 9 : 2 * count + 12]
+    stages, sems = refs[2 * count + 12 : 3 * count + 12], refs[3 * count + 12]
+    d, me, y = lax.axis_index("dp"), lax.axis_index("ctx"), lax.axis_index("fsdp")
+    copies_in = [pltpu.make_async_copy(sources[i], stages[i], sems.at[i]) for i in range(count)]
+    copies_out = [pltpu.make_async_copy(stages[i], targets[i], sems.at[count + i]) for i in range(count)]
+    for copy in copies_in:
+        copy.start()
+
+    def from_lane(values, lane):
+        return pltpu.roll(values, (1024 - lane) % 1024, 1)
+
+    own = from_lane(sums_ref[0:8, :], ((d * 4 + me) * 2 + y) * 32)
+    for i in range(6):
+        rows_out[i][...] = own[i, 0:32]
+    row = lax.broadcasted_iota(jnp.int32, (8, 256), 0)
+    inner = jnp.sum(jnp.where(row == 2 * d + me // 2, sums_ref[8:16, 0:256], 0.0), axis=0, keepdims=True)
+    inner_out[...] = jnp.where(y == 0, inner[:, 0:128], inner[:, 128:256])[0]
+    for start, out in ((0, query_out), (512, value_out)):
+        out[...] = from_lane(sums_ref[16:24, :], start + d * 64 + y * 32)[0, 0:32]
+    for place, out in enumerate(projections):
+        for g in range(4):
+            start = place * 256 + g * 64
+            parts = [qkv_ref[i, :, start : start + 64] for i in range(4)]
+            out[:, g * 256 : g * 256 + 256] = jnp.concatenate(parts, 1)
+    for i in range(count):
+        copies_in[i].wait()
+        copies_out[i].start()
+    for copy in copies_out:
+        copy.wait()
+
+
+def finish_call(sums, qkv_sum, arrays):
+    any_space = pl.BlockSpec(memory_space=pl.ANY)
+    vmem = pl.BlockSpec(memory_space=pltpu.VMEM)
+    short = jax.ShapeDtypeStruct((32,), F32)
+    return pl.pallas_call(
+        finish_kernel,
+        in_specs=[vmem] * 2 + [any_space] * 5,
+        out_specs=[any_space] * 5 + [vmem] * 12,
+        out_shape=[jax.ShapeDtypeStruct(a.shape, a.dtype) for a in arrays]
+        + [short] * 6
+        + [jax.ShapeDtypeStruct((128,), F32), short, short]
+        + [jax.ShapeDtypeStruct((32, 1024), F32)] * 3,
+        scratch_shapes=[pltpu.VMEM(a.shape, a.dtype) for a in arrays] + [pltpu.SemaphoreType.DMA((16,))],
+    )(sums, qkv_sum, *arrays)
+
+
 def shards(
     states,
     cotangent,
@@ -1486,14 +1577,6 @@
         return both_rows[:tokens] + swap(both_rows[tokens:].astype(BF16), "ctx", 1).astype(F32)
 
     if aligned:
-        half_bias = lambda v: pick(v.reshape(2, n_ctx, head_size), me, 1).reshape(1, -1)
-        top = jnp.concatenate((half_bias(query_bias), half_bias(value_bias), jnp.zeros((1, 256), BF16)), 1)
-        rows16 = [top] + [
-            v.reshape(1, -1)
-            for v in (output_bias, first_gain, first_shift, outer_bias, final_gain, final_shift)
-        ]
-        rows16 += [jnp.zeros((1, 512), BF16), inner_bias.reshape(4, 512), jnp.zeros((4, 512), BF16)]
-        vec_own = jnp.concatenate(rows16, 0)
         (
             encoded,
             flat_all,
@@ -1512,10 +1595,32 @@
             slope,
             second_norm,
             second_inverse,
-        ) = layer_call((seq_len, states, wq_own, vec_own, output_weight, inner_weight, outer_weight))
+            own_lengths,
+        ) = layer_call(
+            (
+                lengths,
+                slot_source,
+                states,
+                query_weight,
+                key_weight,
+                value_weight,
+                query_bias,
+                output_bias,
+                first_gain,
+                first_shift,
+                outer_bias,
+                final_gain,
+                final_shift,
+                value_bias,
+                inner_bias,
+                output_weight,
+                inner_weight,
+                outer_weight,
+            )
+        )
         input_grad, outer_weight_own, inner_weight_own, output_weight_own, qkv_sum, sums = back_call(
             (
-                seq_len,
+                own_lengths,
                 cotangent,
                 second_norm,
                 second_inverse,
@@ -1535,33 +1640,30 @@
                 flat_all,
             )
         )
-        rows = width // (8 * n_dp)
-        qkv_sum = qkv_sum.reshape(n_ctx, rows, 3, own_heads, head_size)
-        qkv_sum = jnp.transpose(qkv_sum, (2, 1, 3, 0, 4)).reshape(3, rows, width)
-        spot = ((d * n_ctx + me) * n_fsdp + y) * rows
-        token_sums = lax.dynamic_slice(sums, (0, spot), (6, rows))
-        inner_bias_own = lax.dynamic_slice(sums, (8 + 2 * d + x, y * block // 2), (1, block // 2)).reshape(-1)
-        own_bias = [
-            lax.dynamic_slice(sums, (16, i * cols + d * head_size + y * rows), (1, rows)).reshape(-1) for i in (0, 2)
-        ]
+        finished = finish_call(
+            sums, qkv_sum, (encoded, input_grad, outer_weight_own, inner_weight_own, output_weight_own)
+        )
+        encoded, input_grad, outer_weight_own, inner_weight_own, output_weight_own = finished[:5]
+        final_gain_own, final_shift_own, outer_bias_own, first_gain_own, first_shift_own, output_bias_own = finished[5:11]
+        inner_bias_own, query_bias_own, value_bias_own, query_own, key_own, value_own = finished[11:]
         return (
             encoded.reshape(states.shape),
             input_grad.reshape(states.shape),
-            qkv_sum[0],
-            own_bias[0],
-            qkv_sum[1],
-            qkv_sum[2],
-            own_bias[1],
+            query_own,
+            query_bias_own,
+            key_own,
+            value_own,
+            value_bias_own,
             output_weight_own,
-            token_sums[5],
-            token_sums[3],
-            token_sums[4],
+            output_bias_own,
+            first_gain_own,
+            first_shift_own,
             inner_weight_own,
             inner_bias_own,
             outer_weight_own,
-            token_sums[2],
-            token_sums[0],
-            token_sums[1],
+            outer_bias_own,
+            final_gain_own,
+            final_shift_own,
         )
 
     def other_half(local):

time: 252 us -> 231 us (0.917); the launches traced: 251 us -> 227 us
  local copies, waits for them, and re-layouts: 24.4 us -> 0 us
    reshape x17 -> x0, local copies, waits for them, and re-layouts: 11.5 us -> none  [the longest x6 4.09 us: shards(): v.reshape(1, -1)]
    unnamed x24 -> x0, local copies, waits for them, and re-layouts: 6.84 us -> none
    pallas_call x1, Pallas kernels: 127 us -> 121 us  [back_call(): pl.pallas_call(back_kernel, in_specs=[pl.BlockSpec(memory_space=pltpu.SME...]
    pallas_call x0 -> x1, Pallas kernels: none -> 4.93 us  [finish_call(): pl.pallas_call(finish_kernel, in_specs=[vmem] * 2 + [any_space] * 5, out_...]
    pallas_call x1, Pallas kernels: 96.1 us -> 100 us  [layer_call(): pl.pallas_call(layer_kernel, in_specs=[pl.BlockSpec(memory_space=pltpu.SM...]
    squeeze x4 -> x0, local copies, waits for them, and re-layouts: 3.23 us -> none  [the longest x1 0.9 us: shards(): qkv_sum[2]]
where the time goes in v2:
time: 231 us; the launch traced here: 227 us
  Pallas kernels  226 us (98%)
    pallas_call x1, Pallas kernels, back_call(): pl.pallas_call(back_kernel, in_specs=[pl.BlockSpec(memory_space=pltpu.SME...  121 us
    pallas_call x1, Pallas kernels, layer_call(): pl.pallas_call(layer_kernel, in_specs=[pl.BlockSpec(memory_space=pltpu.SM...  100 us
    pallas_call x1, Pallas kernels, finish_call(): pl.pallas_call(finish_kernel, in_specs=[vmem] * 2 + [any_space] * 5, out_...  4.93 us

profile of v2, /device:TPU:0, one launch (start us, length us, event | category | flops | bytes accessed | tf_op | source)
XLA Modules:
  0.0 227.0 jit_solution(4343274342609761953)
XLA Ops:
  0.7 100.2 %shard_map.314 = (bf16[512,1024]{1,0:T(8,128)(2,1)}, bf16[4,4,128,1024]{3,2,1,0:T(8,128)(2,1)}, bf16[1024,768]{1,0:T(8,128)(2,1)}, bf16[2,4,64,1024]{3,2,1,0:T(8...) custom-call(s32[32]{0:T(128)} %length_ref.1, ...), custom_call_target="tpu_custom_call" | custom-call | tf_op jit(solution)/shard_map/pallas_call | solution.py:656
  100.8 121.1 %shard_map.315 = (bf16[512,1024]{1,0:T(8,128)(2,1)}, f32[128,1024]{1,0:T(8,128)}, f32[32,4096]{1,0:T(8,128)}, f32[32,1024]{1,0:T(8,128)}, f32[4,32,768]{2,1,0:T(8,128)}, /*index=5*/f32[24,1024]{1,0:T(8,128)}) custom-call(s32[4]{0:T(128)} %get-tuple-element.58.lens_ref, bf16[4,128,1024]{2,1,0:T(8,128)(2,1)} %i_cot.1, f32[512,1024]{1,0:T(8,128)} %get-tuple-element.59.i_n2, ...), custom_call_target="tpu_custom_call" | custom-call | tf_op jit(solution)/shard_map/pallas_call | solution.py:1443
  221.9 4.9 %shard_map.316 = (bf16[512,1024]{1,0:T(8,128)(2,1)}, bf16[512,1024]{1,0:T(8,128)(2,1)}, f32[128,1024]{1,0:T(8,128)}, f32[32,4096]{1,0:T(8,128)}, f32[32,1024]{1,...) custom-call(f32[24,1024]{1,0:T(8,128)} %get-tuple-element.75.sums_re, ...), custom_call_target="tpu_custom_call" | custom-call | tf_op jit(solution)/shard_map/pallas_call | solution.py:1499

commit v3 on v2

--- a/solution.py
+++ b/solution.py
@@ -367,9 +367,17 @@
 
     def wu_copy(k):
         side, half = k // 2, k % 2
-        src = wu_own.at[pl.ds(pl.multiple_of((p * 4 + side * 2 + c) * 256 + half * 128, 128), 128)]
-        dst = w_ou.at[pl.ds(pl.multiple_of((4 * y + 2 * p + side) * 256 + half * 128, 128), 128)]
+        start, rows = (0, 128) if half == 0 else (128 + x * 64, 64)
+        src = wu_own.at[pl.ds(pl.multiple_of((p * 4 + side * 2 + c) * 256 + start, 64), rows)]
+        dst = w_ou.at[pl.ds(pl.multiple_of((4 * y + 2 * p + side) * 256 + start, 64), rows)]
         return remote(src, dst, wu_slot + k, to_y)
+
+    wu_side_slot = slots.take(2)
+
+    def wu_side(side):
+        start = (4 * (1 - y) + 2 * p + side) * 256 + 128 + x * 64
+        here = w_ou.at[pl.ds(pl.multiple_of(start, 64), 64)]
+        return remote(here, here, wu_side_slot + side, to_x)
 
     wu_pass_slot = slots.take(4)
 
@@ -392,7 +400,7 @@
         wi_copy(b).start()
     for k in range(4):
         wu_copy(k).start()
-    for count, make in ((2, wo_copy), (2, wo_pass), (8, wi_copy), (8, wi_pass), (4, wu_copy), (4, wu_pass)):
+    for count, make in ((2, wo_copy), (2, wo_pass), (8, wi_copy), (8, wi_pass), (4, wu_copy), (2, wu_side), (4, wu_pass)):
         at_end(count, make)
 
     own_early = [
@@ -560,8 +568,15 @@
 
     repeat(4, norm_first)
 
+    def share_outer(k):
+        wu_copy(k).wait_recv()
+        wu_side(k // 2).start()
+
     def pass_outer(k):
-        wu_copy(k).wait_recv()
+        if k % 2:
+            wu_side(k // 2).wait_recv()
+        else:
+            wu_copy(k).wait_recv()
         wu_pass(k).start()
 
     pass_outer(0)
@@ -573,9 +588,11 @@
         keep(src, dst)
 
     def unit_block(b):
-        @pl.when((b == 2) | (b == 5))
-        def _():
-            pass_outer(1 + b // 4)
+        for step, action, k in ((1, share_outer, 1), (3, pass_outer, 1), (4, pass_outer, 2), (6, share_outer, 3)):
+
+            @pl.when(b == step)
+            def _():
+                action(k)
 
         wi_pass(b).wait_recv()
         here = pl.ds(pl.multiple_of(b * 256, 256), 256)

time: 231 us -> 232 us (level)
  Pallas kernels: 226 us -> 229 us
where the time goes in v3:
time: 232 us; the launch traced here: 230 us
  Pallas kernels  229 us (99%)
    pallas_call x1, Pallas kernels, back_call(): pl.pallas_call(back_kernel, in_specs=[pl.BlockSpec(memory_space=pltpu.SME...  122 us
    pallas_call x1, Pallas kernels, layer_call(): pl.pallas_call(layer_kernel, in_specs=[pl.BlockSpec(memory_space=pltpu.SM...  102 us
    pallas_call x1, Pallas kernels, finish_call(): pl.pallas_call(finish_kernel, in_specs=[vmem] * 2 + [any_space] * 5, out_...  4.93 us

profile of v3, /device:TPU:0, one launch (start us, length us, event | category | flops | bytes accessed | tf_op | source)
XLA Modules:
  0.0 229.6 jit_solution(1335761509880625766)
XLA Ops:
  0.7 101.6 %shard_map.314 = (bf16[512,1024]{1,0:T(8,128)(2,1)}, bf16[4,4,128,1024]{3,2,1,0:T(8,128)(2,1)}, bf16[1024,768]{1,0:T(8,128)(2,1)}, bf16[2,4,64,1024]{3,2,1,0:T(8...) custom-call(s32[32]{0:T(128)} %length_ref.1, ...), custom_call_target="tpu_custom_call" | custom-call | tf_op jit(solution)/shard_map/pallas_call | solution.py:673
  102.3 122.2 %shard_map.315 = (bf16[512,1024]{1,0:T(8,128)(2,1)}, f32[128,1024]{1,0:T(8,128)}, f32[32,4096]{1,0:T(8,128)}, f32[32,1024]{1,0:T(8,128)}, f32[4,32,768]{2,1,0:T(8,128)}, /*index=5*/f32[24,1024]{1,0:T(8,128)}) custom-call(s32[4]{0:T(128)} %get-tuple-element.58.lens_ref, bf16[4,128,1024]{2,1,0:T(8,128)(2,1)} %i_cot.1, f32[512,1024]{1,0:T(8,128)} %get-tuple-element.59.i_n2, ...), custom_call_target="tpu_custom_call" | custom-call | tf_op jit(solution)/shard_map/pallas_call | solution.py:1460
  224.5 4.9 %shard_map.316 = (bf16[512,1024]{1,0:T(8,128)(2,1)}, bf16[512,1024]{1,0:T(8,128)(2,1)}, f32[128,1024]{1,0:T(8,128)}, f32[32,4096]{1,0:T(8,128)}, f32[32,1024]{1,...) custom-call(f32[24,1024]{1,0:T(8,128)} %get-tuple-element.75.sums_re, ...), custom_call_target="tpu_custom_call" | custom-call | tf_op jit(solution)/shard_map/pallas_call | solution.py:1516

commit v4 on v3

--- a/solution.py
+++ b/solution.py
@@ -388,14 +388,14 @@
         ]
         return remote(here, here, wu_pass_slot + k, to_z)
 
-    for side in range(2):
-        wo_copy(side).start()
     for place in range(3):
         three[place].wait()
         made = matmul(own_three[place], chosen[...]).astype(BF16)
         wq_all[pl.ds(pl.multiple_of(y * 512, 512), 512), place * 256 : place * 256 + 256] = made
     for k in range(2):
         wq_copy(k).start()
+    for side in range(2):
+        wo_copy(side).start()
     for b in range(8):
         wi_copy(b).start()
     for k in range(4):
@@ -434,9 +434,6 @@
     vec_copy.wait_recv()
     vecs[:, :512] = vec_all[0]
     vecs[:, 512:] = vec_all[1]
-    for side in range(2):
-        wo_copy(side).wait_recv()
-        wo_pass(side).start()
     for k in range(2):
         wq_pass(k).wait_recv()
 
@@ -469,6 +466,12 @@
         def _():
             state_x(s + 2).wait_recv()
             state_far(s + 2).start()
+
+        @pl.when(s == 1)
+        def _():
+            for side in range(2):
+                wo_copy(side).wait_recv()
+                wo_pass(side).start()
 
         @pl.when((s == 1) | (s == 2))
         def _():

time: 232 us -> 230 us (level)
  Pallas kernels: 229 us -> 225 us
    pallas_call x1, Pallas kernels: 102 us -> 98.1 us  [layer_call(): pl.pallas_call(layer_kernel, in_specs=[pl.BlockSpec(memory_space=pltpu.SM...]
where the time goes in v4:
time: 230 us; the launch traced here: 226 us
  Pallas kernels  225 us (98%)
    pallas_call x1, Pallas kernels, back_call(): pl.pallas_call(back_kernel, in_specs=[pl.BlockSpec(memory_space=pltpu.SME...  122 us
    pallas_call x1, Pallas kernels, layer_call(): pl.pallas_call(layer_kernel, in_specs=[pl.BlockSpec(memory_space=pltpu.SM...  98.1 us
    pallas_call x1, Pallas kernels, finish_call(): pl.pallas_call(finish_kernel, in_specs=[vmem] * 2 + [any_space] * 5, out_...  4.93 us

profile of v4, /device:TPU:0, one launch (start us, length us, event | category | flops | bytes accessed | tf_op | source)
XLA Modules:
  0.0 226.2 jit_solution(18028798963693333007)
XLA Ops:
  0.7 98.1 %shard_map.314 = (bf16[512,1024]{1,0:T(8,128)(2,1)}, bf16[4,4,128,1024]{3,2,1,0:T(8,128)(2,1)}, bf16[1024,768]{1,0:T(8,128)(2,1)}, bf16[2,4,64,1024]{3,2,1,0:T(8...) custom-call(s32[32]{0:T(128)} %length_ref.1, ...), custom_call_target="tpu_custom_call" | custom-call | tf_op jit(solution)/shard_map/pallas_call | solution.py:676
  98.7 122.4 %shard_map.315 = (bf16[512,1024]{1,0:T(8,128)(2,1)}, f32[128,1024]{1,0:T(8,128)}, f32[32,4096]{1,0:T(8,128)}, f32[32,1024]{1,0:T(8,128)}, f32[4,32,768]{2,1,0:T(8,128)}, /*index=5*/f32[24,1024]{1,0:T(8,128)}) custom-call(s32[4]{0:T(128)} %get-tuple-element.58.lens_ref, bf16[4,128,1024]{2,1,0:T(8,128)(2,1)} %i_cot.1, f32[512,1024]{1,0:T(8,128)} %get-tuple-element.59.i_n2, ...), custom_call_target="tpu_custom_call" | custom-call | tf_op jit(solution)/shard_map/pallas_call | solution.py:1463
  221.1 4.9 %shard_map.316 = (bf16[512,1024]{1,0:T(8,128)(2,1)}, bf16[512,1024]{1,0:T(8,128)(2,1)}, f32[128,1024]{1,0:T(8,128)}, f32[32,4096]{1,0:T(8,128)}, f32[32,1024]{1,...) custom-call(f32[24,1024]{1,0:T(8,128)} %get-tuple-element.75.sums_re, ...), custom_call_target="tpu_custom_call" | custom-call | tf_op jit(solution)/shard_map/pallas_call | solution.py:1519
